TPU v7x, 512 devices: a whole 4x8x8 slice. The times are simulated.
512 devices in a mesh: ctx: 32 (over y, x_lo, core), head: 16 (over z, x_hi).
Axes of the slice: x: 4 (x_hi: 2, x_lo: 2; x = x_hi * 2 + x_lo), y: 8, z: 8, core: 2. Of those that a mesh axis runs over, the one named last changes fastest.
Arguments:
- hidden: bfloat16 [2, 4096, 7168], P(None, 'ctx', 'head'), may hold values from -6 to 6
- queries: bfloat16 [2, 4096, 12288], P(None, 'ctx', 'head'), may hold values from -260 to 260
- w_dkv: bfloat16 [7168, 576], P('head'), may hold values from -0.0625 to 0.0625
- kv_gain: float32 [512], replicated, may hold values from 0.1 to 1.9
- w_key: bfloat16 [64, 512, 128], P('head'), may hold values from -0.25 to 0.25
- w_val: bfloat16 [64, 512, 128], P('head'), may hold values from -0.25 to 0.25
- doc_lengths: int32 [16], replicated, may hold values from 1 to 1536, 8192 in all
Outputs:
- attended: bfloat16 [2, 4096, 8192], P(None, 'ctx', 'head')
Inputs may be any that keep to these rules, and one draw needn't show every extreme that they name: `doc_lengths`: lengths sum to 8192; the longest is exactly 1536.
All inputs are finite; a program needn't handle non-finite values.
Results may differ from a plain program's by a relative error of at most 0.02.
The roundings to bfloat16 on the way count: a program that leaves them out, or rounds other values in their place, can miss the bound.
Values may be sent and summed in bfloat16 or wider, within the bound.
A program may use at most 64 MiB of HBM per device.

v0:
```python
import jax
import jax.numpy as jnp
from jax import lax
from jax.sharding import PartitionSpec as P

LATENT = 512
ROPE = 64
NOPE = 128
VDIM = 128
WINDOW = 1024
STEPS = 8


def shifted(value, axis, steps):
    count = lax.axis_size(axis)
    first, last = (max(0, -steps), min(count, count - steps))
    return lax.ppermute(value, axis, [(source, source + steps) for source in range(first, last)])


def rotate(rope_part, positions):
    half_rope = ROPE // 2
    frequency = 10000.0 ** (-jnp.arange(half_rope, dtype=jnp.float32) / half_rope)
    angles = positions.astype(jnp.float32)[:, None] * frequency[None, :]
    cosine = jnp.cos(angles)
    sine_part = jnp.sin(angles)
    front_half = rope_part[:, :half_rope]
    back_half = rope_part[:, half_rope:]
    return jnp.concatenate(
        [front_half * cosine - back_half * sine_part, back_half * cosine + front_half * sine_part],
        1,
    )


def finish_latent(latent, positions, kv_gain):
    compressed = latent[:, :LATENT]
    variance = jnp.mean(compressed * compressed, axis=1, keepdims=True)
    normed = compressed * lax.rsqrt(variance + 1e-06) * kv_gain[None, :]
    rotated = rotate(latent[:, LATENT:], positions)
    return jnp.concatenate([normed, rotated], 1).astype(jnp.bfloat16)


def document_of(positions, doc_lengths):
    bounds = jnp.cumsum(doc_lengths, dtype=jnp.int32)
    return jnp.sum(
        (bounds[None, :] <= positions[:, None]).astype(jnp.int32), axis=1, dtype=jnp.int32
    )


def on_device(hidden, queries, w_dkv, kv_gain, w_key, w_val, doc_lengths):
    ctx_count = lax.axis_size("ctx")
    ctx_index = lax.axis_index("ctx")
    head_local = w_key.shape[0]
    half_rows = hidden.shape[1]
    hidden_rows = hidden.reshape(2 * half_rows, hidden.shape[2])
    offsets = jnp.arange(half_rows, dtype=jnp.int32)
    high_block = 2 * ctx_count - 1 - ctx_index
    positions = jnp.concatenate([ctx_index * half_rows + offsets, high_block * half_rows + offsets])
    partial_value = jnp.dot(hidden_rows, w_dkv, preferred_element_type=jnp.float32)
    latent = lax.psum(partial_value, "head")
    own_keys = finish_latent(latent, positions, kv_gain)
    documents = document_of(positions, doc_lengths)
    query_rows = queries.reshape(2 * half_rows, head_local, NOPE + ROPE)
    absorbed = jnp.einsum(
        "rhn,hln->hrl", query_rows[..., :NOPE], w_key, preferred_element_type=jnp.float32
    ).astype(jnp.bfloat16)
    query_full = jnp.concatenate([absorbed, jnp.transpose(query_rows[..., NOPE:], (1, 0, 2))], 2)
    low_query = query_full[:, :half_rows].reshape(head_local * half_rows, LATENT + ROPE)
    high_query = query_full[:, half_rows:].reshape(head_local * half_rows, LATENT + ROPE)
    low_pos = positions[:half_rows]
    high_pos = positions[half_rows:]
    low_doc = documents[:half_rows]
    high_doc = documents[half_rows:]
    score_scale = (NOPE + ROPE) ** (-0.5)

    def update(state, query_block, query_pos, query_doc, block_keys, key_pos, key_doc):
        run_max, run_sum, run_acc = state
        visible = (key_pos[None, :] <= query_pos[:, None]) & (
            query_pos[:, None] - key_pos[None, :] < WINDOW
        )
        visible = visible & (key_doc[None, :] == query_doc[:, None]) & (key_pos[None, :] >= 0)
        scores = (
            lax.dot_general(
                query_block,
                block_keys,
                (((1,), (1,)), ((), ())),
                preferred_element_type=jnp.float32,
            )
            * score_scale
        )
        scores = scores.reshape(head_local, half_rows, half_rows)
        masked = jnp.where(visible[None], scores, -jnp.inf)
        new_max = jnp.maximum(run_max, jnp.max(masked, axis=2))
        weights = jnp.exp(masked - new_max[..., None]).astype(jnp.bfloat16)
        factor = jnp.exp(run_max - new_max)
        new_sum = run_sum * factor + jnp.sum(weights.astype(jnp.float32), axis=2)
        contrib = jnp.dot(
            weights.reshape(head_local * half_rows, half_rows),
            block_keys[:, :LATENT],
            preferred_element_type=jnp.float32,
        )
        new_acc = run_acc * factor[..., None] + contrib.reshape(head_local, half_rows, LATENT)
        return (new_max, new_sum, new_acc)

    def attend(state, query_block, query_pos, query_doc, block_keys, key_block):
        key_pos = key_block * half_rows + offsets
        key_doc = document_of(jnp.maximum(key_pos, 0), doc_lengths)
        return update(state, query_block, query_pos, query_doc, block_keys, key_pos, key_doc)

    initial = (
        jnp.full((head_local, half_rows), -1e30, jnp.float32),
        jnp.zeros((head_local, half_rows), jnp.float32),
        jnp.zeros((head_local, half_rows, LATENT), jnp.float32),
    )
    low_keys = own_keys[:half_rows]
    high_keys = own_keys[half_rows:]
    low_state = attend(initial, low_query, low_pos, low_doc, low_keys, ctx_index)
    high_state = attend(initial, high_query, high_pos, high_doc, high_keys, high_block)

    def advance(step_index, carry):
        up_buffer, down_buffer, low_carry, high_carry = carry
        up_next = shifted(up_buffer, "ctx", 1)
        down_in = shifted(down_buffer, "ctx", -1)
        down_next = jnp.where(ctx_index == ctx_count - 1, up_buffer, down_in)
        low_carry = attend(low_carry, low_query, low_pos, low_doc, up_next, ctx_index - step_index)
        high_carry = attend(
            high_carry, high_query, high_pos, high_doc, down_next, high_block - step_index
        )
        return (up_next, down_next, low_carry, high_carry)

    finished = lax.fori_loop(1, STEPS + 1, advance, (low_keys, high_keys, low_state, high_state))
    low_state, high_state = (finished[2], finished[3])
    low_mixed = (low_state[2] / low_state[1][..., None]).astype(jnp.bfloat16)
    high_mixed = (high_state[2] / high_state[1][..., None]).astype(jnp.bfloat16)
    stacked = jnp.concatenate([low_mixed, high_mixed], 1)
    values = jnp.einsum("hrl,hlv->rhv", stacked, w_val, preferred_element_type=jnp.float32).astype(
        jnp.bfloat16
    )
    return values.reshape(2, half_rows, head_local * VDIM)


def solution(mesh):
    in_specs = (
        P(None, "ctx", "head"),
        P(None, "ctx", "head"),
        P("head", None),
        P(),
        P("head", None, None),
        P("head", None, None),
        P(),
    )
    out_specs = P(None, "ctx", "head")
    return jax.shard_map(
        on_device, mesh=mesh, in_specs=in_specs, out_specs=out_specs, check_vma=False
    )
```

profile of v0, /device:TPU:27, one launch (start us, length us, event | category | flops | bytes accessed | tf_op | source)
XLA Modules:
  0.0 321.6 jit_solution(196790971779356353)
XLA Ops:
  6.5 1.1 copy-done
  7.6 2.2 fusion.23
  11.8 157.6 %all-reduce.2.cloned.1.call-done = f32[256,576]{0,1:T(8,128)} async-done(((f32[256,576]{0,1:T(8,128)}), f32[256,576]{0,1:T(8,128)}) %all-reduce.2.cloned.1.call-update) | async-done | bytes 589840 | tf_op jit(solution)/shard_map/psum | solution.py:59
  169.5 1.1 multiply_reduce_fusion
  170.6 1.0 fusion.37
  171.6 1.2 multiply_convert_fusion
  172.8 0.8 copy.31
  175.6 1.2 convolution_add_fusion.3
  176.8 135.3 %while.31 = (s32[]{:T(128)}, bf16[128,576]{1,0:T(8,128)(2,1)S(1)}, bf16[128,576]{1,0:T(8,128)(2,1)}, f32[4,128]{1,0:T(4,128)S(1)}, f32[4,128]{1,0:T(4,128)S(1)},...) while((s32[]{:T(128)}, bf16[128,576]{1,0:T(8,128)(2,1)S(1)}, ...), condition=%wide.region_17.18_spmd.clone.clone, body=%wide.region_10.17_spmd.clone.clone.sunk | while | flops 287499520 | bytes 12773334 | solution.py:130
  176.8 0.7 copy.62
  177.5 15.6 %collective-permute-start = (bf16[128,576]{1,0:T(8,128)(2,1)}, bf16[128,576]{1,0:T(8,128)(2,1)S(1)}, u32[]{:S(2)}, u32[]{:S(2)}) collective-permute-start(bf16[128,576]{1,0:T(8,128)(2,1)} %copy.62), channel_id=1, source_target_pairs={{0,16},{16,32},{32,48},{48,64},{64,80},{80,96},{96,112},{112,128},... | collective-permute-start | bytes 442376 | tf_op jit(solution)/shard_map/while/body/eval_jaxpr/ppermute | solution.py:17
  193.1 1.9 collective-permute-start.1
  195.4 6.8 %collective-permute-done.1 = bf16[128,576]{1,0:T(8,128)(2,1)} collective-permute-done((bf16[128,576]{1,0:T(8,128)(2,1)}, bf16[128,576]{1,0:T(8,128)(2,1)}, u32[]{:S(2)}, u32[]{:S(2)}) %collective-permute-start.1) | collective-permute-done | bytes 147488 | tf_op jit(solution)/shard_map/while/body/eval_jaxpr/ppermute | solution.py:17
  202.2 1.0 broadcast_select_fusion.2
  204.7 0.5 convolution_add_fusion.7
  205.2 0.5 convolution_add_fusion.6
  205.7 0.7 copy.62
  206.4 1.9 collective-permute-start
  208.3 2.4 collective-permute-start.1
  211.1 6.3 %collective-permute-done.1 = bf16[128,576]{1,0:T(8,128)(2,1)} collective-permute-done((bf16[128,576]{1,0:T(8,128)(2,1)}, bf16[128,576]{1,0:T(8,128)(2,1)}, u32[]{:S(2)}, u32[]{:S(2)}) %collective-permute-start.1) | collective-permute-done | bytes 147488 | tf_op jit(solution)/shard_map/while/body/eval_jaxpr/ppermute | solution.py:17
  217.4 1.0 broadcast_select_fusion.2
  219.9 0.5 convolution_add_fusion.7
  220.4 0.5 convolution_add_fusion.6
  220.9 0.7 copy.62
  221.6 1.9 collective-permute-start
  223.5 2.4 collective-permute-start.1
  226.3 6.3 %collective-permute-done.1 = bf16[128,576]{1,0:T(8,128)(2,1)} collective-permute-done((bf16[128,576]{1,0:T(8,128)(2,1)}, bf16[128,576]{1,0:T(8,128)(2,1)}, u32[]{:S(2)}, u32[]{:S(2)}) %collective-permute-start.1) | collective-permute-done | bytes 147488 | tf_op jit(solution)/shard_map/while/body/eval_jaxpr/ppermute | solution.py:17
  232.6 1.0 broadcast_select_fusion.2
  235.1 0.5 convolution_add_fusion.7
  235.6 0.5 convolution_add_fusion.6
  236.1 0.7 copy.62
  236.8 1.9 collective-permute-start
  238.7 2.4 collective-permute-start.1
  241.5 6.3 %collective-permute-done.1 = bf16[128,576]{1,0:T(8,128)(2,1)} collective-permute-done((bf16[128,576]{1,0:T(8,128)(2,1)}, bf16[128,576]{1,0:T(8,128)(2,1)}, u32[]{:S(2)}, u32[]{:S(2)}) %collective-permute-start.1) | collective-permute-done | bytes 147488 | tf_op jit(solution)/shard_map/while/body/eval_jaxpr/ppermute | solution.py:17
  247.8 1.0 broadcast_select_fusion.2
  250.3 0.5 convolution_add_fusion.7
  250.8 0.5 convolution_add_fusion.6
  251.3 0.7 copy.62
  252.0 1.9 collective-permute-start
  253.9 2.4 collective-permute-start.1
  256.7 6.3 %collective-permute-done.1 = bf16[128,576]{1,0:T(8,128)(2,1)} collective-permute-done((bf16[128,576]{1,0:T(8,128)(2,1)}, bf16[128,576]{1,0:T(8,128)(2,1)}, u32[]{:S(2)}, u32[]{:S(2)}) %collective-permute-start.1) | collective-permute-done | bytes 147488 | tf_op jit(solution)/shard_map/while/body/eval_jaxpr/ppermute | solution.py:17
  263.0 1.0 broadcast_select_fusion.2
  265.5 0.5 convolution_add_fusion.7
  266.0 0.5 convolution_add_fusion.6
  266.5 0.7 copy.62
  267.2 1.9 collective-permute-start
  269.1 2.4 collective-permute-start.1
  271.9 6.3 %collective-permute-done.1 = bf16[128,576]{1,0:T(8,128)(2,1)} collective-permute-done((bf16[128,576]{1,0:T(8,128)(2,1)}, bf16[128,576]{1,0:T(8,128)(2,1)}, u32[]{:S(2)}, u32[]{:S(2)}) %collective-permute-start.1) | collective-permute-done | bytes 147488 | tf_op jit(solution)/shard_map/while/body/eval_jaxpr/ppermute | solution.py:17
  278.2 1.0 broadcast_select_fusion.2
  281.2 0.5 convolution_add_fusion.6
  281.7 0.7 copy.62
  282.4 1.9 collective-permute-start
  284.3 2.4 collective-permute-start.1
  287.1 6.3 %collective-permute-done.1 = bf16[128,576]{1,0:T(8,128)(2,1)} collective-permute-done((bf16[128,576]{1,0:T(8,128)(2,1)}, bf16[128,576]{1,0:T(8,128)(2,1)}, u32[]{:S(2)}, u32[]{:S(2)}) %collective-permute-start.1) | collective-permute-done | bytes 147488 | tf_op jit(solution)/shard_map/while/body/eval_jaxpr/ppermute | solution.py:17
  293.4 1.0 broadcast_select_fusion.2
  296.4 0.5 convolution_add_fusion.6
  296.9 0.7 copy.62
  297.6 1.9 collective-permute-start
  299.5 2.4 collective-permute-start.1
  302.3 6.3 %collective-permute-done.1 = bf16[128,576]{1,0:T(8,128)(2,1)} collective-permute-done((bf16[128,576]{1,0:T(8,128)(2,1)}, bf16[128,576]{1,0:T(8,128)(2,1)}, u32[]{:S(2)}, u32[]{:S(2)}) %collective-permute-start.1) | collective-permute-done | bytes 147488 | tf_op jit(solution)/shard_map/while/body/eval_jaxpr/ppermute | solution.py:17
  308.6 1.0 broadcast_select_fusion.2
  311.6 0.5 convolution_add_fusion.6
  312.4 0.9 copy-done.8
  314.0 0.8 reshape.693
  (272 shorter events, 20.1 us)
Async XLA Ops:
  6.5 1.1 copy-start
  6.5 3.3 %copy-start.6 = (bf16[2,128,768]{2,1,0:T(8,128)(2,1)S(1)}, bf16[2,128,768]{2,1,0:T(8,128)(2,1)}, u32[]{:S(2)}) copy-start(bf16[2,128,768]{2,1,0:T(8,128)(2,1)} %param.10) | copy-start | bytes 1179652
  6.5 162.9 %all-reduce.2.cloned.1.call-start = ((), (), s32[]{:S(2)}) async-start(), calls=%async_computation | async-start | bytes 1179648 | tf_op jit(solution)/shard_map/psum | solution.py:59
  9.8 0.8 copy-start.9
  9.9 1.1 copy-start.5
  11.5 160.1 %copy-start.7 = (f32[512]{0:T(512)S(1)}, f32[512]{0:T(512)}, u32[]{:S(2)}) copy-start(f32[512]{0:T(512)} %param.12) | copy-start | bytes 6148
  11.6 162.2 %copy-start.1 = (bf16[4,128,576]{2,1,0:T(8,128)(2,1)}, bf16[4,128,576]{2,1,0:T(8,128)(2,1)S(1)}, u32[]{:S(2)}) copy-start(bf16[4,128,576]{2,1,0:T(8,128)(2,1)S(1)} %get-tuple-element.649) | copy-start | bytes 1769476
  172.8 2.5 copy-start.4
  177.5 26.5 %collective-permute-start = (bf16[128,576]{1,0:T(8,128)(2,1)}, bf16[128,576]{1,0:T(8,128)(2,1)S(1)}, u32[]{:S(2)}, u32[]{:S(2)}) collective-permute-start(bf16[128,576]{1,0:T(8,128)(2,1)} %copy.62), channel_id=1, source_target_pairs={{0,16},{16,32},{32,48},{48,64},{64,80},{80,96},{96,112},{112,128},... | collective-permute-start | bytes 442376 | tf_op jit(solution)/shard_map/while/body/eval_jaxpr/ppermute | solution.py:17
  193.1 9.1 %collective-permute-start.1 = (bf16[128,576]{1,0:T(8,128)(2,1)}, bf16[128,576]{1,0:T(8,128)(2,1)}, u32[]{:S(2)}, u32[]{:S(2)}) collective-permute-start(bf16[128,576]{1,0:T(8,128)(2,1)} %get-tuple-element.844), channel_id=1, source_target_pairs={{16,0},{32,16},{48,32},{64,48},{80,64},{96,80},{112,96},{128,112},... | collective-permute-start | bytes 442376 | tf_op jit(solution)/shard_map/while/body/eval_jaxpr/ppermute | solution.py:17
  202.2 1.8 copy-start.2
  203.2 1.5 copy-start.3
  206.4 12.8 %collective-permute-start = (bf16[128,576]{1,0:T(8,128)(2,1)}, bf16[128,576]{1,0:T(8,128)(2,1)S(1)}, u32[]{:S(2)}, u32[]{:S(2)}) collective-permute-start(bf16[128,576]{1,0:T(8,128)(2,1)} %copy.62), channel_id=1, source_target_pairs={{0,16},{16,32},{32,48},{48,64},{64,80},{80,96},{96,112},{112,128},... | collective-permute-start | bytes 442376 | tf_op jit(solution)/shard_map/while/body/eval_jaxpr/ppermute | solution.py:17
  208.3 9.1 %collective-permute-start.1 = (bf16[128,576]{1,0:T(8,128)(2,1)}, bf16[128,576]{1,0:T(8,128)(2,1)}, u32[]{:S(2)}, u32[]{:S(2)}) collective-permute-start(bf16[128,576]{1,0:T(8,128)(2,1)} %get-tuple-element.844), channel_id=1, source_target_pairs={{16,0},{32,16},{48,32},{64,48},{80,64},{96,80},{112,96},{128,112},... | collective-permute-start | bytes 442376 | tf_op jit(solution)/shard_map/while/body/eval_jaxpr/ppermute | solution.py:17
  217.4 1.8 copy-start.2
  218.4 1.5 copy-start.3
  221.6 12.8 %collective-permute-start = (bf16[128,576]{1,0:T(8,128)(2,1)}, bf16[128,576]{1,0:T(8,128)(2,1)S(1)}, u32[]{:S(2)}, u32[]{:S(2)}) collective-permute-start(bf16[128,576]{1,0:T(8,128)(2,1)} %copy.62), channel_id=1, source_target_pairs={{0,16},{16,32},{32,48},{48,64},{64,80},{80,96},{96,112},{112,128},... | collective-permute-start | bytes 442376 | tf_op jit(solution)/shard_map/while/body/eval_jaxpr/ppermute | solution.py:17
  223.5 9.1 %collective-permute-start.1 = (bf16[128,576]{1,0:T(8,128)(2,1)}, bf16[128,576]{1,0:T(8,128)(2,1)}, u32[]{:S(2)}, u32[]{:S(2)}) collective-permute-start(bf16[128,576]{1,0:T(8,128)(2,1)} %get-tuple-element.844), channel_id=1, source_target_pairs={{16,0},{32,16},{48,32},{64,48},{80,64},{96,80},{112,96},{128,112},... | collective-permute-start | bytes 442376 | tf_op jit(solution)/shard_map/while/body/eval_jaxpr/ppermute | solution.py:17
  232.6 1.8 copy-start.2
  233.6 1.5 copy-start.3
  236.8 12.8 %collective-permute-start = (bf16[128,576]{1,0:T(8,128)(2,1)}, bf16[128,576]{1,0:T(8,128)(2,1)S(1)}, u32[]{:S(2)}, u32[]{:S(2)}) collective-permute-start(bf16[128,576]{1,0:T(8,128)(2,1)} %copy.62), channel_id=1, source_target_pairs={{0,16},{16,32},{32,48},{48,64},{64,80},{80,96},{96,112},{112,128},... | collective-permute-start | bytes 442376 | tf_op jit(solution)/shard_map/while/body/eval_jaxpr/ppermute | solution.py:17
  238.7 9.1 %collective-permute-start.1 = (bf16[128,576]{1,0:T(8,128)(2,1)}, bf16[128,576]{1,0:T(8,128)(2,1)}, u32[]{:S(2)}, u32[]{:S(2)}) collective-permute-start(bf16[128,576]{1,0:T(8,128)(2,1)} %get-tuple-element.844), channel_id=1, source_target_pairs={{16,0},{32,16},{48,32},{64,48},{80,64},{96,80},{112,96},{128,112},... | collective-permute-start | bytes 442376 | tf_op jit(solution)/shard_map/while/body/eval_jaxpr/ppermute | solution.py:17
  247.8 1.8 copy-start.2
  248.8 1.5 copy-start.3
  252.0 12.8 %collective-permute-start = (bf16[128,576]{1,0:T(8,128)(2,1)}, bf16[128,576]{1,0:T(8,128)(2,1)S(1)}, u32[]{:S(2)}, u32[]{:S(2)}) collective-permute-start(bf16[128,576]{1,0:T(8,128)(2,1)} %copy.62), channel_id=1, source_target_pairs={{0,16},{16,32},{32,48},{48,64},{64,80},{80,96},{96,112},{112,128},... | collective-permute-start | bytes 442376 | tf_op jit(solution)/shard_map/while/body/eval_jaxpr/ppermute | solution.py:17
  253.9 9.1 %collective-permute-start.1 = (bf16[128,576]{1,0:T(8,128)(2,1)}, bf16[128,576]{1,0:T(8,128)(2,1)}, u32[]{:S(2)}, u32[]{:S(2)}) collective-permute-start(bf16[128,576]{1,0:T(8,128)(2,1)} %get-tuple-element.844), channel_id=1, source_target_pairs={{16,0},{32,16},{48,32},{64,48},{80,64},{96,80},{112,96},{128,112},... | collective-permute-start | bytes 442376 | tf_op jit(solution)/shard_map/while/body/eval_jaxpr/ppermute | solution.py:17
  263.0 1.8 copy-start.2
  264.0 1.5 copy-start.3
  267.2 12.8 %collective-permute-start = (bf16[128,576]{1,0:T(8,128)(2,1)}, bf16[128,576]{1,0:T(8,128)(2,1)S(1)}, u32[]{:S(2)}, u32[]{:S(2)}) collective-permute-start(bf16[128,576]{1,0:T(8,128)(2,1)} %copy.62), channel_id=1, source_target_pairs={{0,16},{16,32},{32,48},{48,64},{64,80},{80,96},{96,112},{112,128},... | collective-permute-start | bytes 442376 | tf_op jit(solution)/shard_map/while/body/eval_jaxpr/ppermute | solution.py:17
  269.1 9.1 %collective-permute-start.1 = (bf16[128,576]{1,0:T(8,128)(2,1)}, bf16[128,576]{1,0:T(8,128)(2,1)}, u32[]{:S(2)}, u32[]{:S(2)}) collective-permute-start(bf16[128,576]{1,0:T(8,128)(2,1)} %get-tuple-element.844), channel_id=1, source_target_pairs={{16,0},{32,16},{48,32},{64,48},{80,64},{96,80},{112,96},{128,112},... | collective-permute-start | bytes 442376 | tf_op jit(solution)/shard_map/while/body/eval_jaxpr/ppermute | solution.py:17
  278.2 1.8 copy-start.2
  279.2 1.5 copy-start.3
  282.4 12.8 %collective-permute-start = (bf16[128,576]{1,0:T(8,128)(2,1)}, bf16[128,576]{1,0:T(8,128)(2,1)S(1)}, u32[]{:S(2)}, u32[]{:S(2)}) collective-permute-start(bf16[128,576]{1,0:T(8,128)(2,1)} %copy.62), channel_id=1, source_target_pairs={{0,16},{16,32},{32,48},{48,64},{64,80},{80,96},{96,112},{112,128},... | collective-permute-start | bytes 442376 | tf_op jit(solution)/shard_map/while/body/eval_jaxpr/ppermute | solution.py:17
  284.3 9.1 %collective-permute-start.1 = (bf16[128,576]{1,0:T(8,128)(2,1)}, bf16[128,576]{1,0:T(8,128)(2,1)}, u32[]{:S(2)}, u32[]{:S(2)}) collective-permute-start(bf16[128,576]{1,0:T(8,128)(2,1)} %get-tuple-element.844), channel_id=1, source_target_pairs={{16,0},{32,16},{48,32},{64,48},{80,64},{96,80},{112,96},{128,112},... | collective-permute-start | bytes 442376 | tf_op jit(solution)/shard_map/while/body/eval_jaxpr/ppermute | solution.py:17
  293.4 1.8 copy-start.2
  294.4 1.5 copy-start.3
  297.6 12.8 %collective-permute-start = (bf16[128,576]{1,0:T(8,128)(2,1)}, bf16[128,576]{1,0:T(8,128)(2,1)S(1)}, u32[]{:S(2)}, u32[]{:S(2)}) collective-permute-start(bf16[128,576]{1,0:T(8,128)(2,1)} %copy.62), channel_id=1, source_target_pairs={{0,16},{16,32},{32,48},{48,64},{64,80},{80,96},{96,112},{112,128},... | collective-permute-start | bytes 442376 | tf_op jit(solution)/shard_map/while/body/eval_jaxpr/ppermute | solution.py:17
  299.5 9.1 %collective-permute-start.1 = (bf16[128,576]{1,0:T(8,128)(2,1)}, bf16[128,576]{1,0:T(8,128)(2,1)}, u32[]{:S(2)}, u32[]{:S(2)}) collective-permute-start(bf16[128,576]{1,0:T(8,128)(2,1)} %get-tuple-element.844), channel_id=1, source_target_pairs={{16,0},{32,16},{48,32},{64,48},{80,64},{96,80},{112,96},{128,112},... | collective-permute-start | bytes 442376 | tf_op jit(solution)/shard_map/while/body/eval_jaxpr/ppermute | solution.py:17
  308.6 1.8 copy-start.2
  309.6 1.5 copy-start.3
  312.3 1.0 copy-start.8
Sparse Core Ops, SparseCore 0:
  10.3 159.1 all-reduce.1
where the time goes:
time: 323 us; the launch traced here: 322 us
  waiting for transfers between devices  209 us (65%)
  starting transfers between devices  47.8 us (15%)
  matrix products  20.2 us (6%)
  other arithmetic  19.4 us (6%)
  between operations  13.7 us (4%)
  local copies, waits for them, and re-layouts  10.4 us (3%)
    psum x1, waiting for transfers between devices, on_device(): latent = lax.psum(partial_value, 'head')  158 us
    ppermute x16, waiting for transfers between devices, shifted(): lax.ppermute(value, axis, [(source, source + steps) for source in range(f...  50.9 us
    ppermute x16, starting transfers between devices, shifted(): lax.ppermute(value, axis, [(source, source + steps) for source in range(f...  47.8 us
    dot_general x18, matrix products, update(): jnp.dot(weights.reshape(head_local * half_rows, half_rows), block_keys[:,...  9.33 us
    select_n x8, other arithmetic, advance(): down_next = jnp.where(ctx_index == ctx_count - 1, up_buffer, down_in)  8.05 us
    dot_general x18, matrix products, update(): lax.dot_general(query_block, block_keys, (((1,), (1,)), ((), ())), prefer...  7.83 us
  transfers between devices with their start and end apart: 17, of which 9 were waited for; matrix products, arithmetic and copies ran while one was open for 6% of the time, Pallas kernels for 0%

commit v1 on v0

v1 whole, which is shorter than its diff:
```python
import functools

import jax
import jax.numpy as jnp
from jax import lax
from jax.experimental import pallas as pl
from jax.experimental.pallas import tpu as pltpu
from jax.sharding import PartitionSpec as P

LATENT = 512
ROPE = 64
NOPE = 128
VDIM = 128
KEY = LATENT + ROPE
WINDOW = 1024
SPAN = 9
BLOCK = 128
ROWS = 16
NEG = -1e30
MESH = pl.DeviceIdType.MESH

OFFSETS = [(dz, dx) for dz in (4, 3, -3, 2, -2, 1, -1, 0) for dx in (0, 1) if (dz, dx) != (0, 0)]
PEERS = len(OFFSETS)


def body(
    hidden_hbm, queries_hbm, w_dkv_hbm, gain_ref, w_key_hbm, w_val_hbm, docs_ref, trig_ref,
    out_ref,
    hidden_v, queries_v, w_dkv_v, w_key_v, w_val_v, part, arrived, keys, qfull, scores, rowmax,
    lower, probs,
    load_sem, rs_send, rs_recv, ag_send, ag_recv, win_send, win_recv,
):
    ctx = lax.axis_index("ctx")
    head = lax.axis_index("head")
    core = ctx % 2
    x_lo = (ctx // 2) % 2
    y = ctx // 4
    col = ctx % 4
    z = head // 2
    x_hi = head % 2
    heads = w_key_v.shape[0]

    def head_peer(dz, dx):
        return ((z + dz + 8) % 8) * 2 + (x_hi + dx) % 2

    same = (x_lo + core + 1) % 2
    down_head = z * 2 + (x_hi + same) % 2
    up_head = z * 2 + (x_hi + 1 - same) % 2
    across_ctx = 4 * y + 2 * (1 - x_lo) + core
    mate_ctx = 4 * y + 2 * x_lo + 1 - core
    mirror_ctx = 4 * y + 3 - col
    last = y // 7
    next_ctx = (1 - last) * (ctx + 4) + last * mirror_ctx

    barrier = pltpu.get_barrier_semaphore()

    def greet(to_ctx, to_head):
        pl.semaphore_signal(barrier, inc=1, device_id=(to_ctx, to_head), device_id_type=MESH)

    for dz, dx in OFFSETS:
        greet(ctx, head_peer(dz, dx))
    greet((ctx + 4) % 32, head)
    greet((ctx + 28) % 32, head)
    greet(mirror_ctx, head)
    greet(mate_ctx, head)
    greet(across_ctx, down_head)
    greet(across_ctx, up_head)

    loads = [
        pltpu.make_async_copy(source, target, load_sem.at[i])
        for i, (source, target) in enumerate(
            [
                (hidden_hbm, hidden_v),
                (w_dkv_hbm, w_dkv_v),
                (queries_hbm, queries_v),
                (w_key_hbm, w_key_v),
                (w_val_hbm, w_val_v),
            ]
        )
    ]
    for load in loads:
        load.start()
    loads[0].wait()
    loads[1].wait()
    for half in range(2):
        part[half * BLOCK : (half + 1) * BLOCK, :] = jnp.dot(
            hidden_v[half], w_dkv_v[...], preferred_element_type=jnp.float32
        )

    pl.semaphore_wait(barrier, PEERS + 6)

    rs = []
    for i, (dz, dx) in enumerate(OFFSETS):
        peer = head_peer(dz, dx)
        copy = pltpu.make_async_remote_copy(
            src_ref=part.at[pl.ds(pl.multiple_of(peer * ROWS, ROWS), ROWS), :],
            dst_ref=arrived.at[i],
            send_sem=rs_send.at[i],
            recv_sem=rs_recv.at[i],
            device_id=(ctx, peer),
            device_id_type=MESH,
        )
        copy.start()
        rs.append(copy)

    row = lax.broadcasted_iota(jnp.int32, (BLOCK, BLOCK), 0)
    lane = lax.broadcasted_iota(jnp.int32, (BLOCK, BLOCK), 1)
    for half in range(2):
        query_block = ctx if half == 0 else 63 - ctx
        position = query_block * BLOCK + row
        start = jnp.zeros((BLOCK, BLOCK), jnp.int32)
        bound = jnp.int32(0)
        for i in range(docs_ref.shape[0]):
            bound = bound + docs_ref[i]
            start = jnp.maximum(start, jnp.where(bound <= position, bound, 0))
        lower[half] = jnp.maximum(start - (query_block - (SPAN - 1)) * BLOCK, row + 1)

    loads[2].wait()
    loads[3].wait()
    for half in range(2):
        for n in range(heads):
            at = n * (NOPE + ROPE)
            rows = slice(n * BLOCK, (n + 1) * BLOCK)
            qfull[half, rows, :LATENT] = lax.dot_general(
                queries_v[half, :, at : at + NOPE],
                w_key_v[n],
                (((1,), (1,)), ((), ())),
                preferred_element_type=jnp.float32,
            ).astype(jnp.bfloat16)
            qfull[half, rows, LATENT:] = queries_v[half, :, at + NOPE : at + NOPE + ROPE]

    @pl.when(y == 0)
    def _():
        keys[0, 0] = jnp.zeros((BLOCK, KEY), jnp.bfloat16)
        keys[0, 4] = jnp.zeros((BLOCK, KEY), jnp.bfloat16)

    for copy in reversed(rs):
        copy.wait_recv()
    latent = part[pl.ds(pl.multiple_of(head * ROWS, ROWS), ROWS), :]
    for i in range(PEERS):
        latent = latent + arrived[i]
    compressed = latent[:, :LATENT]
    variance = jnp.mean(compressed * compressed, axis=1, keepdims=True)
    normed = compressed * lax.rsqrt(variance + 1e-06) * gain_ref[...]
    front, back = latent[:, LATENT : LATENT + ROPE // 2], latent[:, LATENT + ROPE // 2 :]
    cosine, sine = trig_ref[0], trig_ref[1]
    rotated = jnp.concatenate([front * cosine - back * sine, back * cosine + front * sine], 1)

    def piece(of_head):
        return keys.at[of_head // 8, 8, pl.ds(pl.multiple_of(of_head % 8 * ROWS, ROWS), ROWS), :]

    keys[head // 8, 8, pl.ds(pl.multiple_of(head % 8 * ROWS, ROWS), ROWS), :] = jnp.concatenate(
        [normed, rotated], 1
    ).astype(jnp.bfloat16)

    ag = []
    for i, (dz, dx) in enumerate(OFFSETS):
        copy = pltpu.make_async_remote_copy(
            src_ref=piece(head),
            dst_ref=piece(head),
            send_sem=ag_send.at[i],
            recv_sem=ag_recv.at[i],
            device_id=(ctx, head_peer(dz, dx)),
            device_id_type=MESH,
        )
        copy.start()
        ag.append(copy)
    for i, (dz, dx) in reversed(list(enumerate(OFFSETS))):
        come = piece(head_peer(-dz, dx))
        pltpu.make_async_remote_copy(
            src_ref=come,
            dst_ref=come,
            send_sem=ag_send.at[i],
            recv_sem=ag_recv.at[i],
            device_id=(ctx, head_peer(-dz, dx)),
            device_id_type=MESH,
        ).wait_recv()

    sent = []

    def send(condition, half, index, to_half, to_index, to_ctx, to_head):
        copy = pltpu.make_async_remote_copy(
            src_ref=keys.at[half, index],
            dst_ref=keys.at[to_half, to_index],
            send_sem=win_send.at[len(sent)],
            recv_sem=win_recv.at[to_half, to_index],
            device_id=(to_ctx, to_head),
            device_id_type=MESH,
        )
        sent.append((condition, copy))
        if condition is None:
            copy.start()
        else:
            pl.when(condition)(copy.start)

    def take(half, index):
        pltpu.make_async_remote_copy(
            src_ref=keys.at[half, index],
            dst_ref=keys.at[half, index],
            send_sem=win_send.at[0],
            recv_sem=win_recv.at[half, index],
            device_id=(ctx, head),
            device_id_type=MESH,
        ).wait_recv()

    def score(half, index):
        raw = lax.dot_general(
            qfull[half], keys[half, index], (((1,), (1,)), ((), ())), preferred_element_type=jnp.float32
        )
        seen = index * BLOCK + lane >= lower[half]
        if index == SPAN - 1:
            seen = seen & (lane <= row)
        masked = jnp.where(seen[None], raw.reshape(heads, BLOCK, BLOCK), NEG).reshape(heads * BLOCK, BLOCK)
        scores[half, index] = masked
        if index == SPAN - 1:
            rowmax[half] = masked
        else:
            rowmax[half] = jnp.maximum(rowmax[half], masked)

    first = y == 0
    onward = y > 0
    send(None, 0, 8, last, 4, next_ctx, head)
    send(onward, 1, 8, 1, 4, ctx - 4, head)
    send(x_lo == 0, 0, 8, 0, 6, across_ctx, down_head)
    send(x_lo == 1, 1, 8, 1, 6, across_ctx, down_head)
    send(core == 0, 0, 8, 0, 7, mate_ctx, head)
    send(core == 1, 1, 8, 1, 7, mate_ctx, head)
    score(0, 8)
    score(1, 8)

    pl.when(onward)(functools.partial(take, 0, 4))
    send(None, 0, 4, last, 0, next_ctx, head)
    send(None, 0, 4, 0, 2 + 4 * x_lo, across_ctx, down_head)
    send(None, 0, 4, 0, 3 + 2 * core, mate_ctx, head)
    take(1, 4)
    send(onward, 1, 4, 1, 0, ctx - 4, head)
    send(None, 1, 4, 1, 6 - 4 * x_lo, across_ctx, down_head)
    send(None, 1, 4, 1, 5 - 2 * core, mate_ctx, head)
    score(0, 4)
    score(1, 4)

    for half in range(2):
        take(half, 6)
        send(None, half, 6, half, 5 + 2 * core if half == 0 else 7 - 2 * core, mate_ctx, head)
    score(0, 6)
    score(1, 6)

    pl.when(onward)(functools.partial(take, 0, 0))
    send(x_lo == 1, 0, 0, 0, 2, across_ctx, down_head)
    send(core == 1, 0, 0, 0, 1, mate_ctx, head)
    take(1, 0)
    send(x_lo == 0, 1, 0, 1, 2, across_ctx, down_head)
    send(core == 0, 1, 0, 1, 1, mate_ctx, head)
    score(0, 0)
    score(1, 0)

    for half in range(2):
        take(half, 2)
        send(None, half, 2, half, 1 + 2 * core if half == 0 else 3 - 2 * core, mate_ctx, head)
    score(0, 2)
    score(1, 2)
    for index in (7, 5, 3, 1):
        for half in range(2):
            take(half, index)
            score(half, index)

    loads[4].wait()
    to_log2 = (NOPE + ROPE) ** -0.5 * 1.4426950408889634
    for half in range(2):
        top = jnp.max(rowmax[half], axis=1, keepdims=True)
        total = jnp.zeros((heads * BLOCK, BLOCK), jnp.float32)
        for index in range(SPAN):
            weight = jnp.exp2((scores[half, index] - top) * to_log2).astype(jnp.bfloat16)
            probs[:, index * BLOCK : (index + 1) * BLOCK] = weight
            total = total + weight.astype(jnp.float32)
        denominator = jnp.sum(total, axis=1, keepdims=True)
        values = keys[half].reshape(SPAN * BLOCK, KEY)[:, :LATENT]
        numerator = jnp.dot(probs[...], values, preferred_element_type=jnp.float32)
        mixed = (numerator * (1.0 / denominator)).astype(jnp.bfloat16)
        for n in range(heads):
            out_ref[half, :, n * VDIM : (n + 1) * VDIM] = jnp.dot(
                mixed[n * BLOCK : (n + 1) * BLOCK], w_val_v[n], preferred_element_type=jnp.float32
            ).astype(jnp.bfloat16)

    for copy in rs + ag:
        copy.wait_send()
    for condition, copy in sent:
        if condition is None:
            copy.wait_send()
        else:
            pl.when(condition)(copy.wait_send)


def on_device(hidden, queries, w_dkv, kv_gain, w_key, w_val, doc_lengths):
    ctx = lax.axis_index("ctx")
    head = lax.axis_index("head")
    heads = w_key.shape[0]
    block = jnp.where(head < 8, ctx, 63 - ctx)
    positions = block * BLOCK + head % 8 * ROWS + jnp.arange(ROWS, dtype=jnp.int32)
    half_rope = ROPE // 2
    frequency = 10000.0 ** (-jnp.arange(half_rope, dtype=jnp.float32) / half_rope)
    angles = positions.astype(jnp.float32)[:, None] * frequency[None, :]
    trig = jnp.stack([jnp.cos(angles), jnp.sin(angles)])
    any_space = pl.BlockSpec(memory_space=pl.ANY)
    in_vmem = pl.BlockSpec(memory_space=pltpu.VMEM)
    bf16, f32 = jnp.bfloat16, jnp.float32
    dma = pltpu.SemaphoreType.DMA
    return pl.pallas_call(
        body,
        out_shape=jax.ShapeDtypeStruct((2, BLOCK, heads * VDIM), bf16),
        in_specs=[any_space, any_space, any_space, in_vmem, any_space, any_space,
                  pl.BlockSpec(memory_space=pltpu.SMEM), in_vmem],
        out_specs=in_vmem,
        scratch_shapes=[
            pltpu.VMEM(hidden.shape, bf16),
            pltpu.VMEM(queries.shape, bf16),
            pltpu.VMEM(w_dkv.shape, bf16),
            pltpu.VMEM(w_key.shape, bf16),
            pltpu.VMEM(w_val.shape, bf16),
            pltpu.VMEM((2 * BLOCK, KEY), f32),
            pltpu.VMEM((PEERS, ROWS, KEY), f32),
            pltpu.VMEM((2, SPAN, BLOCK, KEY), bf16),
            pltpu.VMEM((2, heads * BLOCK, KEY), bf16),
            pltpu.VMEM((2, SPAN, heads * BLOCK, BLOCK), f32),
            pltpu.VMEM((2, heads * BLOCK, BLOCK), f32),
            pltpu.VMEM((2, BLOCK, BLOCK), jnp.int32),
            pltpu.VMEM((heads * BLOCK, SPAN * BLOCK), bf16),
            dma((5,)), dma((PEERS,)), dma((PEERS,)), dma((PEERS,)), dma((PEERS,)),
            dma((24,)), dma((2, SPAN)),
        ],
        compiler_params=pltpu.CompilerParams(
            collective_id=0, has_side_effects=True, vmem_limit_bytes=60 * 1024 * 1024
        ),
    )(hidden, queries, w_dkv, kv_gain.reshape(1, LATENT), w_key, w_val, doc_lengths, trig)


def solution(mesh):
    in_specs = (
        P(None, "ctx", "head"),
        P(None, "ctx", "head"),
        P("head", None),
        P(),
        P("head", None, None),
        P("head", None, None),
        P(),
    )
    out_specs = P(None, "ctx", "head")
    return jax.shard_map(
        on_device, mesh=mesh, in_specs=in_specs, out_specs=out_specs, check_vma=False
    )
```

time: 323 us -> 69.6 us (0.22)
  the two profiles are of different devices: /device:TPU:27 before, /device:TPU:8 now
where the time goes in v1:
time: 69.6 us; the launch traced here: 69.4 us
  Pallas kernels  65.2 us (94%)
  local copies, waits for them, and re-layouts  3.45 us (5%)
  other arithmetic  0.73 us (1%)
    pallas_call x1, Pallas kernels, on_device(): pl.pallas_call(body, out_shape=jax.ShapeDtypeStruct((2, BLOCK, heads * VD...  65.2 us
    unnamed x2, local copies, waits for them, and re-layouts  3.45 us

profile of v1, /device:TPU:8, one launch (start us, length us, event | category | flops | bytes accessed | tf_op | source)
XLA Modules:
  0.0 69.4 jit_solution(12229929076985037860)
XLA Ops:
  0.0 0.1 multiply_cosine_fusion
  0.1 0.6 pad_maximum_fusion.trig_ref
  0.7 1.8 %copy.8.hidden_hbm = bf16[2,128,448]{2,1,0:T(8,128)(2,1)} copy(bf16[2,128,448]{1,2,0:T(8,128)(2,1)} %param.7) | data formatting | bytes 458752 | tf_op args[0]
  2.5 65.2 %shard_map.73 = bf16[2,128,512]{2,1,0:T(8,128)(2,1)} custom-call(bf16[2,128,448]{2,1,0:T(8,128)(2,1)} %copy.8.hidden_hbm, bf16[2,128,768]{2,1,0:T(8,128)(2,1)} %queries_hbm.1, bf16[448,576]{1,0:T(8,128)(2,1)} %w_dkv_hbm.1, f32[1,512]{1,0:T(1,128)} %bitcast.1, bf16[4,512,128]{2,1,0:T(8,128)(2,1)} %w_key_hbm.1, bf16[4,512,128]{2,1,0:T(8,128)(2,1)} %w_val_hbm.1, ...), custom_call_target="tpu_custom_call" | custom-call | tf_op jit(solution)/shard_map/pallas_call | solution.py:308
  67.7 1.7 %copy.10 = bf16[2,128,512]{2,1,0:T(8,128)(2,1)} copy(bf16[2,128,512]{2,1,0:T(8,128)(2,1)} %shard_map.73) | data formatting | bytes 524288
  (2 shorter events, 0.0 us)

commit v2 on v1

v2 whole, which is shorter than its diff:
```python
import functools

import jax
import jax.numpy as jnp
import numpy as np
from jax import lax
from jax.experimental import pallas as pl
from jax.experimental.pallas import tpu as pltpu
from jax.sharding import PartitionSpec as P

LATENT = 512
ROPE = 64
NOPE = 128
VDIM = 128
KEY = LATENT + ROPE
WINDOW = 1024
SPAN = 9
BLOCK = 128
ROWS = 16
CHUNK = 64
PARTS = BLOCK // CHUNK
AHEAD = 4
BEHIND = 3
NEG = -1e30
MESH = pl.DeviceIdType.MESH

OFFSETS = [(dz, dx) for dz in (4, 3, -3, 2, -2, 1, -1, 0) for dx in (0, 1) if (dz, dx) != (0, 0)]
PEERS = len(OFFSETS)


def body(
    hidden_hbm, queries_hbm, w_dkv_hbm, gain_hbm, w_key_hbm, w_val_hbm, docs_hbm, turn_block_hbm, turn_row_hbm,
    out_ref,
    hidden_v, queries_v, w_dkv_v, gain_v, w_key_v, w_val_v, docs_s, turn_block_v, turn_row_v,
    part, forward, backward, crossed, keys, qfull, scores, rowmax, lower, probs,
    load_sem, fw_send, fw_recv, bw_send, bw_recv, cross_sem, ag_send, ag_recv, win_send, win_recv,
):
    ctx = lax.axis_index("ctx")
    head = lax.axis_index("head")
    core = ctx % 2
    x_lo = (ctx // 2) % 2
    y = ctx // 4
    col = ctx % 4
    z = head // 2
    x_hi = head % 2
    heads = w_key_v.shape[0]

    def head_peer(dz, dx):
        return ((z + dz + 8) % 8) * 2 + (x_hi + dx) % 2

    same = (x_lo + core + 1) % 2
    down_head = z * 2 + (x_hi + same) % 2
    up_head = z * 2 + (x_hi + 1 - same) % 2
    across_ctx = 4 * y + 2 * (1 - x_lo) + core
    mate_ctx = 4 * y + 2 * x_lo + 1 - core
    mirror_ctx = 4 * y + 3 - col
    last = y // 7
    next_ctx = (1 - last) * (ctx + 4) + last * mirror_ctx
    next_head = (1 - last) * head + last * down_head

    barrier = pltpu.get_barrier_semaphore()

    def greet(to_ctx, to_head):
        pl.semaphore_signal(barrier, inc=1, device_id=(to_ctx, to_head), device_id_type=MESH)

    greet(ctx, head_peer(1, 0))
    greet(ctx, head_peer(-1, 0))
    greet(ctx, head_peer(0, 1))
    greet(across_ctx, down_head)
    greet(across_ctx, up_head)
    greet((ctx + 4) % 32, head)
    greet((ctx + 28) % 32, head)
    greet(mirror_ctx, down_head)
    greet(mate_ctx, head)

    loads = [
        pltpu.make_async_copy(source, target, load_sem.at[i])
        for i, (source, target) in enumerate(
            [
                (hidden_hbm, hidden_v),
                (w_dkv_hbm, w_dkv_v),
                (queries_hbm, queries_v),
                (w_key_hbm, w_key_v),
                (w_val_hbm, w_val_v),
                (docs_hbm, docs_s),
                (gain_hbm, gain_v),
                (turn_block_hbm, turn_block_v),
                (turn_row_hbm, turn_row_v),
            ]
        )
    ]
    for load in loads:
        load.start()
    loads[0].wait()
    loads[1].wait()
    for half in range(2):
        part[half * BLOCK : (half + 1) * BLOCK, :] = lax.dot_general(
            hidden_v[half], w_dkv_v[...], (((0,), (0,)), ((), ())), preferred_element_type=jnp.float32
        )

    pl.semaphore_wait(barrier, 9)

    def rows_of(dz, dx):
        return pl.ds(pl.multiple_of(head_peer(dz, dx) * ROWS, ROWS), ROWS)

    def pass_on(step, dx, ahead):
        i = dx * AHEAD + step
        copy = pltpu.make_async_remote_copy(
            src_ref=part.at[rows_of(AHEAD - step if ahead else step - BEHIND, dx), :],
            dst_ref=(forward if ahead else backward).at[i],
            send_sem=(fw_send if ahead else bw_send).at[i],
            recv_sem=(fw_recv if ahead else bw_recv).at[i],
            device_id=(ctx, head_peer(1 if ahead else -1, 0)),
            device_id_type=MESH,
        )
        copy.start()
        return copy

    rs = {}
    for dx in (1, 0):
        rs[0, dx, True] = pass_on(0, dx, True)
        rs[0, dx, False] = pass_on(0, dx, False)

    def collect(step, dx, ahead):
        i = dx * AHEAD + step
        rs[step, dx, ahead].wait_recv()
        rows = rows_of(AHEAD - 1 - step if ahead else step + 1 - BEHIND, dx)
        part[rows, :] = part[rows, :] + (forward if ahead else backward)[i]

    row = lax.broadcasted_iota(jnp.int32, (BLOCK, BLOCK), 0)
    lane = lax.broadcasted_iota(jnp.int32, (BLOCK, BLOCK), 1)

    def bounds():
        loads[5].wait()
        for half in range(2):
            query_block = ctx if half == 0 else 63 - ctx
            position = query_block * BLOCK + row
            start = jnp.zeros((BLOCK, BLOCK), jnp.int32)
            bound = jnp.int32(0)
            for i in range(docs_s.shape[0]):
                bound = bound + docs_s[i]
                start = jnp.maximum(start, jnp.where(bound <= position, bound, 0))
            lower[half] = jnp.maximum(start - (query_block - (SPAN - 1)) * BLOCK, row + 1)

    def absorb(half):
        for n in range(heads):
            at = n * (NOPE + ROPE)
            rows = slice(n * BLOCK, (n + 1) * BLOCK)
            qfull[half, rows, :LATENT] = lax.dot_general(
                queries_v[half, :, at : at + NOPE],
                w_key_v[n],
                (((1,), (1,)), ((), ())),
                preferred_element_type=jnp.float32,
            ).astype(jnp.bfloat16)
            qfull[half, rows, LATENT:] = queries_v[half, :, at + NOPE : at + NOPE + ROPE]

    def fill(step):
        if step == 0:
            bounds()
        elif step == 1:
            loads[2].wait()
            loads[3].wait()
            absorb(0)
        else:
            absorb(1)

    @pl.when(y == 0)
    def _():
        keys[0, 0] = jnp.zeros((BLOCK, KEY), jnp.bfloat16)
        keys[0, 4] = jnp.zeros((BLOCK, KEY), jnp.bfloat16)

    for step in range(AHEAD - 1):
        fill(step)
        for dx in (1, 0):
            collect(step, dx, True)
            rs[step + 1, dx, True] = pass_on(step + 1, dx, True)
            if step < BEHIND - 1:
                collect(step, dx, False)
                rs[step + 1, dx, False] = pass_on(step + 1, dx, False)
    collect(BEHIND - 1, 1, False)
    collect(AHEAD - 1, 1, True)
    cross = pltpu.make_async_remote_copy(
        src_ref=part.at[rows_of(0, 1), :],
        dst_ref=crossed,
        send_sem=cross_sem.at[0],
        recv_sem=cross_sem.at[1],
        device_id=(ctx, head_peer(0, 1)),
        device_id_type=MESH,
    )
    cross.start()
    collect(BEHIND - 1, 0, False)
    collect(AHEAD - 1, 0, True)
    for i in (6, 7, 8):
        loads[i].wait()
    key_block = (1 - head // 8) * ctx + head // 8 * (63 - ctx)
    by_block = turn_block_v[pl.ds(key_block, 1), :]
    by_row = turn_row_v[pl.ds(pl.multiple_of(head % 8 * ROWS, ROWS), ROWS), :]
    quarter = ROPE // 2
    cos_a, sin_a = by_block[:, :quarter], by_block[:, quarter:]
    cos_b, sin_b = by_row[:, :quarter], by_row[:, quarter:]
    cosine = cos_a * cos_b - sin_a * sin_b
    sine = sin_a * cos_b + cos_a * sin_b

    cross.wait_recv()
    latent = part[rows_of(0, 0), :] + crossed[...]
    compressed = latent[:, :LATENT]
    variance = jnp.mean(compressed * compressed, axis=1, keepdims=True)
    normed = compressed * lax.rsqrt(variance + 1e-06) * gain_v[...]
    front, back = latent[:, LATENT : LATENT + quarter], latent[:, LATENT + quarter :]
    rotated = jnp.concatenate([front * cosine - back * sine, back * cosine + front * sine], 1)

    def piece(of_head):
        return keys.at[of_head // 8, 8, pl.ds(pl.multiple_of(of_head % 8 * ROWS, ROWS), ROWS), :]

    keys[head // 8, 8, pl.ds(pl.multiple_of(head % 8 * ROWS, ROWS), ROWS), :] = jnp.concatenate(
        [normed, rotated], 1
    ).astype(jnp.bfloat16)

    ag = []
    for i, (dz, dx) in enumerate(OFFSETS):
        copy = pltpu.make_async_remote_copy(
            src_ref=piece(head),
            dst_ref=piece(head),
            send_sem=ag_send.at[i],
            recv_sem=ag_recv.at[head],
            device_id=(ctx, head_peer(dz, dx)),
            device_id_type=MESH,
        )
        copy.start()
        ag.append(copy)

    def gathered(half, part_index):
        for i in range(CHUNK // ROWS):
            of_head = half * 8 + part_index * (CHUNK // ROWS) + i

            @pl.when(head != of_head)
            def _():
                pltpu.make_async_remote_copy(
                    src_ref=piece(of_head),
                    dst_ref=piece(of_head),
                    send_sem=ag_send.at[0],
                    recv_sem=ag_recv.at[of_head],
                    device_id=(ctx, head_peer(1, 0)),
                    device_id_type=MESH,
                ).wait_recv()

    sent = []

    def chunk(half, index, u):
        return keys.at[half, index, pl.ds(u * CHUNK, CHUNK), :]

    def send(condition, half, index, u, to_half, to_index, to_ctx, to_head):
        copy = pltpu.make_async_remote_copy(
            src_ref=chunk(half, index, u),
            dst_ref=chunk(to_half, to_index, u),
            send_sem=win_send.at[len(sent)],
            recv_sem=win_recv.at[to_half, to_index, u],
            device_id=(to_ctx, to_head),
            device_id_type=MESH,
        )
        sent.append((condition, copy))
        if condition is None:
            copy.start()
        else:
            pl.when(condition)(copy.start)

    def take(half, index, u):
        pltpu.make_async_remote_copy(
            src_ref=chunk(half, index, u),
            dst_ref=chunk(half, index, u),
            send_sem=win_send.at[0],
            recv_sem=win_recv.at[half, index, u],
            device_id=(mate_ctx, head),
            device_id_type=MESH,
        ).wait_recv()

    def score(half, index):
        raw = lax.dot_general(
            qfull[half], keys[half, index], (((1,), (1,)), ((), ())), preferred_element_type=jnp.float32
        )
        seen = index * BLOCK + lane >= lower[half]
        if index == SPAN - 1:
            seen = seen & (lane <= row)
        masked = jnp.where(seen[None], raw.reshape(heads, BLOCK, BLOCK), NEG).reshape(heads * BLOCK, BLOCK)
        scores[half, index] = masked
        if index == SPAN - 1:
            rowmax[half] = masked
        else:
            rowmax[half] = jnp.maximum(rowmax[half], masked)

    onward = y > 0
    for u in range(PARTS):
        gathered(0, u)
        send(None, 0, 8, u, last, 4, next_ctx, next_head)
        send(x_lo == 0, 0, 8, u, 0, 6, across_ctx, down_head)
        send(core == 0, 0, 8, u, 0, 7, mate_ctx, head)
    for u in range(PARTS):
        gathered(1, u)
        send(onward, 1, 8, u, 1, 4, ctx - 4, head)
        send(x_lo == 1, 1, 8, u, 1, 6, across_ctx, down_head)
        send(core == 1, 1, 8, u, 1, 7, mate_ctx, head)
    score(0, 8)
    score(1, 8)

    for u in range(PARTS):
        pl.when(onward)(functools.partial(take, 0, 4, u))
        send(None, 0, 4, u, last, 0, next_ctx, next_head)
        send(None, 0, 4, u, 0, 2 + 4 * x_lo, across_ctx, down_head)
        send(None, 0, 4, u, 0, 3 + 2 * core, mate_ctx, head)
        take(1, 4, u)
        send(onward, 1, 4, u, 1, 0, ctx - 4, head)
        send(None, 1, 4, u, 1, 6 - 4 * x_lo, across_ctx, down_head)
        send(None, 1, 4, u, 1, 5 - 2 * core, mate_ctx, head)
    score(0, 4)
    score(1, 4)

    for u in range(PARTS):
        for half in range(2):
            take(half, 6, u)
            send(None, half, 6, u, half, 5 + 2 * core if half == 0 else 7 - 2 * core, mate_ctx, head)
    score(0, 6)
    score(1, 6)

    for u in range(PARTS):
        pl.when(onward)(functools.partial(take, 0, 0, u))
        send(x_lo == 1, 0, 0, u, 0, 2, across_ctx, down_head)
        send(core == 1, 0, 0, u, 0, 1, mate_ctx, head)
        take(1, 0, u)
        send(x_lo == 0, 1, 0, u, 1, 2, across_ctx, down_head)
        send(core == 0, 1, 0, u, 1, 1, mate_ctx, head)
    score(0, 0)
    score(1, 0)

    for u in range(PARTS):
        for half in range(2):
            take(half, 2, u)
            send(None, half, 2, u, half, 1 + 2 * core if half == 0 else 3 - 2 * core, mate_ctx, head)
    score(0, 2)
    score(1, 2)
    for index in (7, 5, 3, 1):
        for half in range(2):
            for u in range(PARTS):
                take(half, index, u)
            score(half, index)

    loads[4].wait()
    to_log2 = (NOPE + ROPE) ** -0.5 * 1.4426950408889634
    for half in range(2):
        top = jnp.max(rowmax[half], axis=1, keepdims=True)
        total = jnp.zeros((heads * BLOCK, BLOCK), jnp.float32)
        for index in range(SPAN):
            weight = jnp.exp2((scores[half, index] - top) * to_log2).astype(jnp.bfloat16)
            probs[:, index * BLOCK : (index + 1) * BLOCK] = weight
            total = total + weight.astype(jnp.float32)
        denominator = jnp.sum(total, axis=1, keepdims=True)
        values = keys[half].reshape(SPAN * BLOCK, KEY)[:, :LATENT]
        numerator = jnp.dot(probs[...], values, preferred_element_type=jnp.float32)
        mixed = (numerator * (1.0 / denominator)).astype(jnp.bfloat16)
        for n in range(heads):
            out_ref[half, :, n * VDIM : (n + 1) * VDIM] = jnp.dot(
                mixed[n * BLOCK : (n + 1) * BLOCK], w_val_v[n], preferred_element_type=jnp.float32
            ).astype(jnp.bfloat16)

    for copy in [*rs.values(), cross, *ag]:
        copy.wait_send()
    for condition, copy in sent:
        if condition is None:
            copy.wait_send()
        else:
            pl.when(condition)(copy.wait_send)


def turns(positions):
    angles = positions[:, None] * 10000.0 ** (-np.arange(ROPE // 2) / (ROPE // 2))[None, :]
    return np.concatenate([np.cos(angles), np.sin(angles)], 1).astype(np.float32)


def on_device(hidden, queries, w_dkv, kv_gain, w_key, w_val, doc_lengths):
    heads = w_key.shape[0]
    hidden = jnp.swapaxes(hidden, 1, 2)
    turn_block = jnp.asarray(turns(np.arange(64) * BLOCK))
    turn_row = jnp.asarray(turns(np.arange(BLOCK)))
    any_space = pl.BlockSpec(memory_space=pl.ANY)
    in_vmem = pl.BlockSpec(memory_space=pltpu.VMEM)
    bf16, f32 = jnp.bfloat16, jnp.float32
    dma = pltpu.SemaphoreType.DMA
    return pl.pallas_call(
        body,
        out_shape=jax.ShapeDtypeStruct((2, BLOCK, heads * VDIM), bf16),
        in_specs=[any_space] * 9,
        out_specs=in_vmem,
        scratch_shapes=[
            pltpu.VMEM(hidden.shape, bf16),
            pltpu.VMEM(queries.shape, bf16),
            pltpu.VMEM(w_dkv.shape, bf16),
            pltpu.VMEM((1, LATENT), f32),
            pltpu.VMEM(w_key.shape, bf16),
            pltpu.VMEM(w_val.shape, bf16),
            pltpu.SMEM(doc_lengths.shape, jnp.int32),
            pltpu.VMEM(turn_block.shape, f32),
            pltpu.VMEM(turn_row.shape, f32),
            pltpu.VMEM((2 * BLOCK, KEY), f32),
            pltpu.VMEM((2 * AHEAD, ROWS, KEY), f32),
            pltpu.VMEM((2 * AHEAD, ROWS, KEY), f32),
            pltpu.VMEM((ROWS, KEY), f32),
            pltpu.VMEM((2, SPAN, BLOCK, KEY), bf16),
            pltpu.VMEM((2, heads * BLOCK, KEY), bf16),
            pltpu.VMEM((2, SPAN, heads * BLOCK, BLOCK), f32),
            pltpu.VMEM((2, heads * BLOCK, BLOCK), f32),
            pltpu.VMEM((2, BLOCK, BLOCK), jnp.int32),
            pltpu.VMEM((heads * BLOCK, SPAN * BLOCK), bf16),
            dma((9,)), dma((2 * AHEAD,)), dma((2 * AHEAD,)), dma((2 * AHEAD,)), dma((2 * AHEAD,)), dma((2,)),
            dma((PEERS,)), dma((PEERS + 1,)), dma((40,)), dma((2, SPAN, PARTS)),
        ],
        compiler_params=pltpu.CompilerParams(
            collective_id=0, has_side_effects=True, vmem_limit_bytes=60 * 1024 * 1024
        ),
    )(hidden, queries, w_dkv, kv_gain.reshape(1, LATENT), w_key, w_val, doc_lengths, turn_block, turn_row)


def solution(mesh):
    in_specs = (
        P(None, "ctx", "head"),
        P(None, "ctx", "head"),
        P("head", None),
        P(),
        P("head", None, None),
        P("head", None, None),
        P(),
    )
    out_specs = P(None, "ctx", "head")
    return jax.shard_map(
        on_device, mesh=mesh, in_specs=in_specs, out_specs=out_specs, check_vma=False
    )
```

time: 69.6 us -> 61.1 us (0.88)
  the two profiles are of different devices: /device:TPU:8 before, /device:TPU:56 now
where the time goes in v2:
time: 61.1 us; the launch traced here: 60.9 us
  Pallas kernels  59.2 us (97%)
  local copies, waits for them, and re-layouts  1.67 us (3%)
    pallas_call x1, Pallas kernels, on_device(): pl.pallas_call(body, out_shape=jax.ShapeDtypeStruct((2, BLOCK, heads * VD...  59.2 us
    unnamed x1, local copies, waits for them, and re-layouts  1.67 us

profile of v2, /device:TPU:56, one launch (start us, length us, event | category | flops | bytes accessed | tf_op | source)
XLA Modules:
  0.0 60.9 jit_solution(4964938947738440234)
XLA Ops:
  0.0 59.2 %shard_map.91 = bf16[2,128,512]{2,1,0:T(8,128)(2,1)} custom-call(bf16[2,448,128]{2,1,0:T(8,128)(2,1)} %bitcast.2, bf16[2,128,768]{2,1,0:T(8,128)(2,1)} %queries_hbm.1, bf16[448,576]{1,0:T(8,128)(2,1)} %w_dkv_hbm.1, f32[1,512]{1,0:T(1,128)} %bitcast.3, bf16[4,512,128]{2,1,0:T(8,128)(2,1)} %w_key_hbm.1, bf16[4,512,128]{2,1,0:T(8,128)(2,1)} %w_val_hbm.1, ...), custom_call_target="tpu_custom_call" | custom-call | tf_op jit(solution)/shard_map/pallas_call | solution.py:387
  59.2 1.7 %copy.11 = bf16[2,128,512]{2,1,0:T(8,128)(2,1)} copy(bf16[2,128,512]{2,1,0:T(8,128)(2,1)} %shard_map.91) | data formatting | bytes 524288

commit v3 on v2

--- a/solution.py
+++ b/solution.py
@@ -19,8 +19,9 @@
 ROWS = 16
 CHUNK = 64
 PARTS = BLOCK // CHUNK
-AHEAD = 4
-BEHIND = 3
+REACH = 3
+SLOT = {8: 0, 4: 1, 0: 2, 6: 3, 2: 4, 7: 5, 5: 6, 1: 7, 3: 8}
+EARLY = 4
 NEG = -1e30
 MESH = pl.DeviceIdType.MESH
 
@@ -32,8 +33,8 @@
     hidden_hbm, queries_hbm, w_dkv_hbm, gain_hbm, w_key_hbm, w_val_hbm, docs_hbm, turn_block_hbm, turn_row_hbm,
     out_ref,
     hidden_v, queries_v, w_dkv_v, gain_v, w_key_v, w_val_v, docs_s, turn_block_v, turn_row_v,
-    part, forward, backward, crossed, keys, qfull, scores, rowmax, lower, probs,
-    load_sem, fw_send, fw_recv, bw_send, bw_recv, cross_sem, ag_send, ag_recv, win_send, win_recv,
+    part, forward, backward, opposite, crossed, keys, qfull, scores, rowmax, lower, probs, top_early, total_early, mixing,
+    load_sem, fw_send, fw_recv, bw_send, bw_recv, op_send, op_recv, cross_sem, ag_send, ag_recv, win_send, win_recv,
 ):
     ctx = lax.axis_index("ctx")
     head = lax.axis_index("head")
@@ -65,6 +66,7 @@
 
     greet(ctx, head_peer(1, 0))
     greet(ctx, head_peer(-1, 0))
+    greet(ctx, head_peer(4, 0))
     greet(ctx, head_peer(0, 1))
     greet(across_ctx, down_head)
     greet(across_ctx, up_head)
@@ -89,28 +91,30 @@
             ]
         )
     ]
-    for load in loads:
-        load.start()
+    loads[0].start()
+    loads[1].start()
     loads[0].wait()
     loads[1].wait()
+    for load in loads[2:]:
+        load.start()
     for half in range(2):
         part[half * BLOCK : (half + 1) * BLOCK, :] = lax.dot_general(
             hidden_v[half], w_dkv_v[...], (((0,), (0,)), ((), ())), preferred_element_type=jnp.float32
         )
 
-    pl.semaphore_wait(barrier, 9)
+    pl.semaphore_wait(barrier, 10)
 
     def rows_of(dz, dx):
         return pl.ds(pl.multiple_of(head_peer(dz, dx) * ROWS, ROWS), ROWS)
 
-    def pass_on(step, dx, ahead):
-        i = dx * AHEAD + step
+    def pass_on(step, dx, way):
+        i = dx * REACH + step
         copy = pltpu.make_async_remote_copy(
-            src_ref=part.at[rows_of(AHEAD - step if ahead else step - BEHIND, dx), :],
-            dst_ref=(forward if ahead else backward).at[i],
-            send_sem=(fw_send if ahead else bw_send).at[i],
-            recv_sem=(fw_recv if ahead else bw_recv).at[i],
-            device_id=(ctx, head_peer(1 if ahead else -1, 0)),
+            src_ref=part.at[rows_of(way * (REACH - step), dx), :],
+            dst_ref=(forward if way == 1 else backward).at[i],
+            send_sem=(fw_send if way == 1 else bw_send).at[i],
+            recv_sem=(fw_recv if way == 1 else bw_recv).at[i],
+            device_id=(ctx, head_peer(way, 0)),
             device_id_type=MESH,
         )
         copy.start()
@@ -118,14 +122,34 @@
 
     rs = {}
     for dx in (1, 0):
-        rs[0, dx, True] = pass_on(0, dx, True)
-        rs[0, dx, False] = pass_on(0, dx, False)
-
-    def collect(step, dx, ahead):
-        i = dx * AHEAD + step
-        rs[step, dx, ahead].wait_recv()
-        rows = rows_of(AHEAD - 1 - step if ahead else step + 1 - BEHIND, dx)
-        part[rows, :] = part[rows, :] + (forward if ahead else backward)[i]
+        for way in (1, -1):
+            rs[0, dx, way] = pass_on(0, dx, way)
+    straight = []
+    for dx in (1, 0):
+        copy = pltpu.make_async_remote_copy(
+            src_ref=part.at[rows_of(4, dx), :],
+            dst_ref=opposite.at[dx],
+            send_sem=op_send.at[dx],
+            recv_sem=op_recv.at[dx],
+            device_id=(ctx, head_peer(4, 0)),
+            device_id_type=MESH,
+        )
+        copy.start()
+        straight.append(copy)
+
+    def collect(step, dx, way):
+        i = dx * REACH + step
+        rs[step, dx, way].wait_recv()
+        rows = rows_of(way * (REACH - 1 - step), dx)
+        part[rows, :] = part[rows, :] + (forward if way == 1 else backward)[i]
+
+    def collect_all(dx):
+        for way in (1, -1):
+            rs[REACH - 1, dx, way].wait_recv()
+        straight[1 - dx].wait_recv()
+        i = dx * REACH + REACH - 1
+        rows = rows_of(0, dx)
+        part[rows, :] = part[rows, :] + forward[i] + (backward[i] + opposite[dx])
 
     row = lax.broadcasted_iota(jnp.int32, (BLOCK, BLOCK), 0)
     lane = lax.broadcasted_iota(jnp.int32, (BLOCK, BLOCK), 1)
@@ -166,19 +190,17 @@
 
     @pl.when(y == 0)
     def _():
-        keys[0, 0] = jnp.zeros((BLOCK, KEY), jnp.bfloat16)
-        keys[0, 4] = jnp.zeros((BLOCK, KEY), jnp.bfloat16)
-
-    for step in range(AHEAD - 1):
+        keys[0, SLOT[0]] = jnp.zeros((BLOCK, KEY), jnp.bfloat16)
+        keys[0, SLOT[4]] = jnp.zeros((BLOCK, KEY), jnp.bfloat16)
+
+    for step in range(REACH - 1):
         fill(step)
         for dx in (1, 0):
-            collect(step, dx, True)
-            rs[step + 1, dx, True] = pass_on(step + 1, dx, True)
-            if step < BEHIND - 1:
-                collect(step, dx, False)
-                rs[step + 1, dx, False] = pass_on(step + 1, dx, False)
-    collect(BEHIND - 1, 1, False)
-    collect(AHEAD - 1, 1, True)
+            for way in (1, -1):
+                collect(step, dx, way)
+                rs[step + 1, dx, way] = pass_on(step + 1, dx, way)
+    fill(REACH - 1)
+    collect_all(1)
     cross = pltpu.make_async_remote_copy(
         src_ref=part.at[rows_of(0, 1), :],
         dst_ref=crossed,
@@ -188,8 +210,7 @@
         device_id_type=MESH,
     )
     cross.start()
-    collect(BEHIND - 1, 0, False)
-    collect(AHEAD - 1, 0, True)
+    collect_all(0)
     for i in (6, 7, 8):
         loads[i].wait()
     key_block = (1 - head // 8) * ctx + head // 8 * (63 - ctx)
@@ -210,9 +231,9 @@
     rotated = jnp.concatenate([front * cosine - back * sine, back * cosine + front * sine], 1)
 
     def piece(of_head):
-        return keys.at[of_head // 8, 8, pl.ds(pl.multiple_of(of_head % 8 * ROWS, ROWS), ROWS), :]
-
-    keys[head // 8, 8, pl.ds(pl.multiple_of(head % 8 * ROWS, ROWS), ROWS), :] = jnp.concatenate(
+        return keys.at[of_head // 8, SLOT[8], pl.ds(pl.multiple_of(of_head % 8 * ROWS, ROWS), ROWS), :]
+
+    keys[head // 8, SLOT[8], pl.ds(pl.multiple_of(head % 8 * ROWS, ROWS), ROWS), :] = jnp.concatenate(
         [normed, rotated], 1
     ).astype(jnp.bfloat16)
 
@@ -249,6 +270,9 @@
     def chunk(half, index, u):
         return keys.at[half, index, pl.ds(u * CHUNK, CHUNK), :]
 
+    def either(bit, index, other):
+        return SLOT[index] * (1 - bit) + SLOT[other] * bit
+
     def send(condition, half, index, u, to_half, to_index, to_ctx, to_head):
         copy = pltpu.make_async_remote_copy(
             src_ref=chunk(half, index, u),
@@ -274,94 +298,111 @@
             device_id_type=MESH,
         ).wait_recv()
 
-    def score(half, index):
-        raw = lax.dot_general(
-            qfull[half], keys[half, index], (((1,), (1,)), ((), ())), preferred_element_type=jnp.float32
-        )
-        seen = index * BLOCK + lane >= lower[half]
-        if index == SPAN - 1:
-            seen = seen & (lane <= row)
-        masked = jnp.where(seen[None], raw.reshape(heads, BLOCK, BLOCK), NEG).reshape(heads * BLOCK, BLOCK)
-        scores[half, index] = masked
-        if index == SPAN - 1:
-            rowmax[half] = masked
-        else:
-            rowmax[half] = jnp.maximum(rowmax[half], masked)
+    place = {slot: index for index, slot in SLOT.items()}
+
+    def score(first, count):
+        for half in range(2):
+            block_keys = keys[half, first : first + count].reshape(count * BLOCK, KEY)
+            raw = lax.dot_general(
+                qfull[half], block_keys, (((1,), (1,)), ((), ())), preferred_element_type=jnp.float32
+            )
+            highest = None if first == 0 else rowmax[half]
+            for i in range(count):
+                index = place[first + i]
+                seen = index * BLOCK + lane >= lower[half]
+                if index == SPAN - 1:
+                    seen = seen & (lane <= row)
+                own = raw[:, i * BLOCK : (i + 1) * BLOCK].reshape(heads, BLOCK, BLOCK)
+                masked = jnp.where(seen[None], own, NEG).reshape(heads * BLOCK, BLOCK)
+                scores[half, first + i] = masked
+                highest = masked if highest is None else jnp.maximum(highest, masked)
+            rowmax[half] = highest
+
+    to_log2 = (NOPE + ROPE) ** -0.5 * 1.4426950408889634
+
+    def weigh(half, first, count, top, total):
+        for slot in range(first, first + count):
+            weight = jnp.exp2((scores[half, slot] - top) * to_log2).astype(jnp.bfloat16)
+            probs[:, slot * BLOCK : (slot + 1) * BLOCK] = weight
+            total = total + weight.astype(jnp.float32)
+        values = keys[half, first : first + count].reshape(count * BLOCK, KEY)[:, :LATENT]
+        return total, jnp.dot(
+            probs[:, first * BLOCK : (first + count) * BLOCK], values, preferred_element_type=jnp.float32
+        )
 
     onward = y > 0
     for u in range(PARTS):
         gathered(0, u)
-        send(None, 0, 8, u, last, 4, next_ctx, next_head)
-        send(x_lo == 0, 0, 8, u, 0, 6, across_ctx, down_head)
-        send(core == 0, 0, 8, u, 0, 7, mate_ctx, head)
+        send(None, 0, SLOT[8], u, last, SLOT[4], next_ctx, next_head)
+        send(x_lo == 0, 0, SLOT[8], u, 0, SLOT[6], across_ctx, down_head)
+        send(core == 0, 0, SLOT[8], u, 0, SLOT[7], mate_ctx, head)
     for u in range(PARTS):
         gathered(1, u)
-        send(onward, 1, 8, u, 1, 4, ctx - 4, head)
-        send(x_lo == 1, 1, 8, u, 1, 6, across_ctx, down_head)
-        send(core == 1, 1, 8, u, 1, 7, mate_ctx, head)
-    score(0, 8)
-    score(1, 8)
-
-    for u in range(PARTS):
-        pl.when(onward)(functools.partial(take, 0, 4, u))
-        send(None, 0, 4, u, last, 0, next_ctx, next_head)
-        send(None, 0, 4, u, 0, 2 + 4 * x_lo, across_ctx, down_head)
-        send(None, 0, 4, u, 0, 3 + 2 * core, mate_ctx, head)
-        take(1, 4, u)
-        send(onward, 1, 4, u, 1, 0, ctx - 4, head)
-        send(None, 1, 4, u, 1, 6 - 4 * x_lo, across_ctx, down_head)
-        send(None, 1, 4, u, 1, 5 - 2 * core, mate_ctx, head)
-    score(0, 4)
-    score(1, 4)
-
-    for u in range(PARTS):
-        for half in range(2):
-            take(half, 6, u)
-            send(None, half, 6, u, half, 5 + 2 * core if half == 0 else 7 - 2 * core, mate_ctx, head)
-    score(0, 6)
-    score(1, 6)
-
-    for u in range(PARTS):
-        pl.when(onward)(functools.partial(take, 0, 0, u))
-        send(x_lo == 1, 0, 0, u, 0, 2, across_ctx, down_head)
-        send(core == 1, 0, 0, u, 0, 1, mate_ctx, head)
-        take(1, 0, u)
-        send(x_lo == 0, 1, 0, u, 1, 2, across_ctx, down_head)
-        send(core == 0, 1, 0, u, 1, 1, mate_ctx, head)
-    score(0, 0)
-    score(1, 0)
-
-    for u in range(PARTS):
-        for half in range(2):
-            take(half, 2, u)
-            send(None, half, 2, u, half, 1 + 2 * core if half == 0 else 3 - 2 * core, mate_ctx, head)
-    score(0, 2)
-    score(1, 2)
-    for index in (7, 5, 3, 1):
-        for half in range(2):
-            for u in range(PARTS):
-                take(half, index, u)
-            score(half, index)
-
-    loads[4].wait()
-    to_log2 = (NOPE + ROPE) ** -0.5 * 1.4426950408889634
+        send(onward, 1, SLOT[8], u, 1, SLOT[4], ctx - 4, head)
+        send(x_lo == 1, 1, SLOT[8], u, 1, SLOT[6], across_ctx, down_head)
+        send(core == 1, 1, SLOT[8], u, 1, SLOT[7], mate_ctx, head)
+    score(SLOT[8], 1)
+
+    for u in range(PARTS):
+        pl.when(onward)(functools.partial(take, 0, SLOT[4], u))
+        send(None, 0, SLOT[4], u, last, SLOT[0], next_ctx, next_head)
+        send(None, 0, SLOT[4], u, 0, either(x_lo, 2, 6), across_ctx, down_head)
+        send(None, 0, SLOT[4], u, 0, either(core, 3, 5), mate_ctx, head)
+        take(1, SLOT[4], u)
+        send(onward, 1, SLOT[4], u, 1, SLOT[0], ctx - 4, head)
+        send(None, 1, SLOT[4], u, 1, either(x_lo, 6, 2), across_ctx, down_head)
+        send(None, 1, SLOT[4], u, 1, either(core, 5, 3), mate_ctx, head)
+    score(SLOT[4], 1)
+
+    for u in range(PARTS):
+        pl.when(onward)(functools.partial(take, 0, SLOT[0], u))
+        send(x_lo == 1, 0, SLOT[0], u, 0, SLOT[2], across_ctx, down_head)
+        send(core == 1, 0, SLOT[0], u, 0, SLOT[1], mate_ctx, head)
+        take(1, SLOT[0], u)
+        send(x_lo == 0, 1, SLOT[0], u, 1, SLOT[2], across_ctx, down_head)
+        send(core == 0, 1, SLOT[0], u, 1, SLOT[1], mate_ctx, head)
+    for u in range(PARTS):
+        for half in range(2):
+            take(half, SLOT[6], u)
+            to = either(core, 5, 7) if half == 0 else either(core, 7, 5)
+            send(None, half, SLOT[6], u, half, to, mate_ctx, head)
+    score(SLOT[0], 2)
     for half in range(2):
         top = jnp.max(rowmax[half], axis=1, keepdims=True)
-        total = jnp.zeros((heads * BLOCK, BLOCK), jnp.float32)
-        for index in range(SPAN):
-            weight = jnp.exp2((scores[half, index] - top) * to_log2).astype(jnp.bfloat16)
-            probs[:, index * BLOCK : (index + 1) * BLOCK] = weight
-            total = total + weight.astype(jnp.float32)
-        denominator = jnp.sum(total, axis=1, keepdims=True)
-        values = keys[half].reshape(SPAN * BLOCK, KEY)[:, :LATENT]
-        numerator = jnp.dot(probs[...], values, preferred_element_type=jnp.float32)
-        mixed = (numerator * (1.0 / denominator)).astype(jnp.bfloat16)
+        top_early[half] = jnp.broadcast_to(top, (heads * BLOCK, BLOCK))
+        total_early[half], mixing[half] = weigh(
+            half, 0, EARLY, top, jnp.zeros((heads * BLOCK, BLOCK), jnp.float32)
+        )
+
+    for u in range(PARTS):
+        for half in range(2):
+            take(half, SLOT[2], u)
+            to = either(core, 1, 3) if half == 0 else either(core, 3, 1)
+            send(None, half, SLOT[2], u, half, to, mate_ctx, head)
+    for index in (7, 5):
+        for half in range(2):
+            for u in range(PARTS):
+                take(half, SLOT[index], u)
+    score(SLOT[2], 3)
+    for index in (1, 3):
+        for half in range(2):
+            for u in range(PARTS):
+                take(half, SLOT[index], u)
+    score(SLOT[1], 2)
+
+    loads[4].wait()
+    for half in range(2):
+        top = jnp.max(rowmax[half], axis=1, keepdims=True)
+        fade = jnp.exp2((top_early[half] - top) * to_log2)
+        total, numerator = weigh(half, EARLY, SPAN - EARLY, top, total_early[half] * fade)
+        numerator = numerator + mixing[half] * fade[:, :1]
+        mixed = (numerator * (1.0 / jnp.sum(total, axis=1, keepdims=True))).astype(jnp.bfloat16)
         for n in range(heads):
             out_ref[half, :, n * VDIM : (n + 1) * VDIM] = jnp.dot(
                 mixed[n * BLOCK : (n + 1) * BLOCK], w_val_v[n], preferred_element_type=jnp.float32
             ).astype(jnp.bfloat16)
 
-    for copy in [*rs.values(), cross, *ag]:
+    for copy in [*rs.values(), *straight, cross, *ag]:
         copy.wait_send()
     for condition, copy in sent:
         if condition is None:
@@ -400,8 +441,9 @@
             pltpu.VMEM(turn_block.shape, f32),
             pltpu.VMEM(turn_row.shape, f32),
             pltpu.VMEM((2 * BLOCK, KEY), f32),
-            pltpu.VMEM((2 * AHEAD, ROWS, KEY), f32),
-            pltpu.VMEM((2 * AHEAD, ROWS, KEY), f32),
+            pltpu.VMEM((2 * REACH, ROWS, KEY), f32),
+            pltpu.VMEM((2 * REACH, ROWS, KEY), f32),
+            pltpu.VMEM((2, ROWS, KEY), f32),
             pltpu.VMEM((ROWS, KEY), f32),
             pltpu.VMEM((2, SPAN, BLOCK, KEY), bf16),
             pltpu.VMEM((2, heads * BLOCK, KEY), bf16),
@@ -409,7 +451,10 @@
             pltpu.VMEM((2, heads * BLOCK, BLOCK), f32),
             pltpu.VMEM((2, BLOCK, BLOCK), jnp.int32),
             pltpu.VMEM((heads * BLOCK, SPAN * BLOCK), bf16),
-            dma((9,)), dma((2 * AHEAD,)), dma((2 * AHEAD,)), dma((2 * AHEAD,)), dma((2 * AHEAD,)), dma((2,)),
+            pltpu.VMEM((2, heads * BLOCK, BLOCK), f32),
+            pltpu.VMEM((2, heads * BLOCK, BLOCK), f32),
+            pltpu.VMEM((2, heads * BLOCK, LATENT), f32),
+            dma((9,)), dma((2 * REACH,)), dma((2 * REACH,)), dma((2 * REACH,)), dma((2 * REACH,)), dma((2,)), dma((2,)), dma((2,)),
             dma((PEERS,)), dma((PEERS + 1,)), dma((40,)), dma((2, SPAN, PARTS)),
         ],
         compiler_params=pltpu.CompilerParams(

time: 61.1 us -> 57.2 us (0.936)
  the two profiles are of different devices: /device:TPU:56 before, /device:TPU:19 now
where the time goes in v3:
time: 57.2 us; the launch traced here: 57.1 us
  Pallas kernels  55.4 us (97%)
  local copies, waits for them, and re-layouts  1.67 us (3%)
    pallas_call x1, Pallas kernels, on_device(): pl.pallas_call(body, out_shape=jax.ShapeDtypeStruct((2, BLOCK, heads * VD...  55.4 us
    unnamed x1, local copies, waits for them, and re-layouts  1.67 us

profile of v3, /device:TPU:19, one launch (start us, length us, event | category | flops | bytes accessed | tf_op | source)
XLA Modules:
  0.0 57.1 jit_solution(1008956461022669261)
XLA Ops:
  0.0 55.4 %shard_map.91 = bf16[2,128,512]{2,1,0:T(8,128)(2,1)} custom-call(bf16[2,448,128]{2,1,0:T(8,128)(2,1)} %bitcast.2, bf16[2,128,768]{2,1,0:T(8,128)(2,1)} %queries_hbm.1, bf16[448,576]{1,0:T(8,128)(2,1)} %w_dkv_hbm.1, f32[1,512]{1,0:T(1,128)} %bitcast.3, bf16[4,512,128]{2,1,0:T(8,128)(2,1)} %w_key_hbm.1, bf16[4,512,128]{2,1,0:T(8,128)(2,1)} %w_val_hbm.1, ...), custom_call_target="tpu_custom_call" | custom-call | tf_op jit(solution)/shard_map/pallas_call | solution.py:428
  55.4 1.7 %copy.11 = bf16[2,128,512]{2,1,0:T(8,128)(2,1)} copy(bf16[2,128,512]{2,1,0:T(8,128)(2,1)} %shard_map.91) | data formatting | bytes 524288

commit v4 on v3

--- a/solution.py
+++ b/solution.py
@@ -19,22 +19,22 @@
 ROWS = 16
 CHUNK = 64
 PARTS = BLOCK // CHUNK
-REACH = 3
 SLOT = {8: 0, 4: 1, 0: 2, 6: 3, 2: 4, 7: 5, 5: 6, 1: 7, 3: 8}
 EARLY = 4
 NEG = -1e30
 MESH = pl.DeviceIdType.MESH
 
-OFFSETS = [(dz, dx) for dz in (4, 3, -3, 2, -2, 1, -1, 0) for dx in (0, 1) if (dz, dx) != (0, 0)]
-PEERS = len(OFFSETS)
+NEAR = [(dz, dx) for dz in (2, -2, 1, -1, 0) for dx in (1, 0) if (dz, dx) != (0, 0)]
+PEERS = 15
+ALONG = (4, 3, -3, 2, -2, 1, -1, 0)
 
 
 def body(
     hidden_hbm, queries_hbm, w_dkv_hbm, gain_hbm, w_key_hbm, w_val_hbm, docs_hbm, turn_block_hbm, turn_row_hbm,
     out_ref,
     hidden_v, queries_v, w_dkv_v, gain_v, w_key_v, w_val_v, docs_s, turn_block_v, turn_row_v,
-    part, forward, backward, opposite, crossed, keys, qfull, scores, rowmax, lower, probs, top_early, total_early, mixing,
-    load_sem, fw_send, fw_recv, bw_send, bw_recv, op_send, op_recv, cross_sem, ag_send, ag_recv, win_send, win_recv,
+    part, crossed, arrived, keys, qfull, scores, rowmax, lower, probs, top_early, total_early, mixing,
+    load_sem, cross_send, cross_recv, rs_send, rs_recv, ag_send, ag_recv, win_send, win_recv,
 ):
     ctx = lax.axis_index("ctx")
     head = lax.axis_index("head")
@@ -64,10 +64,9 @@
     def greet(to_ctx, to_head):
         pl.semaphore_signal(barrier, inc=1, device_id=(to_ctx, to_head), device_id_type=MESH)
 
-    greet(ctx, head_peer(1, 0))
-    greet(ctx, head_peer(-1, 0))
-    greet(ctx, head_peer(4, 0))
     greet(ctx, head_peer(0, 1))
+    for dz in ALONG[:-1]:
+        greet(ctx, head_peer(dz, 0))
     greet(across_ctx, down_head)
     greet(across_ctx, up_head)
     greet((ctx + 4) % 32, head)
@@ -102,54 +101,23 @@
             hidden_v[half], w_dkv_v[...], (((0,), (0,)), ((), ())), preferred_element_type=jnp.float32
         )
 
-    pl.semaphore_wait(barrier, 10)
+    pl.semaphore_wait(barrier, len(ALONG) + 6)
 
     def rows_of(dz, dx):
         return pl.ds(pl.multiple_of(head_peer(dz, dx) * ROWS, ROWS), ROWS)
 
-    def pass_on(step, dx, way):
-        i = dx * REACH + step
+    cross = []
+    for i, dz in enumerate(ALONG):
         copy = pltpu.make_async_remote_copy(
-            src_ref=part.at[rows_of(way * (REACH - step), dx), :],
-            dst_ref=(forward if way == 1 else backward).at[i],
-            send_sem=(fw_send if way == 1 else bw_send).at[i],
-            recv_sem=(fw_recv if way == 1 else bw_recv).at[i],
-            device_id=(ctx, head_peer(way, 0)),
+            src_ref=part.at[rows_of(dz, 1), :],
+            dst_ref=crossed.at[i],
+            send_sem=cross_send.at[i],
+            recv_sem=cross_recv.at[i],
+            device_id=(ctx, head_peer(0, 1)),
             device_id_type=MESH,
         )
         copy.start()
-        return copy
-
-    rs = {}
-    for dx in (1, 0):
-        for way in (1, -1):
-            rs[0, dx, way] = pass_on(0, dx, way)
-    straight = []
-    for dx in (1, 0):
-        copy = pltpu.make_async_remote_copy(
-            src_ref=part.at[rows_of(4, dx), :],
-            dst_ref=opposite.at[dx],
-            send_sem=op_send.at[dx],
-            recv_sem=op_recv.at[dx],
-            device_id=(ctx, head_peer(4, 0)),
-            device_id_type=MESH,
-        )
-        copy.start()
-        straight.append(copy)
-
-    def collect(step, dx, way):
-        i = dx * REACH + step
-        rs[step, dx, way].wait_recv()
-        rows = rows_of(way * (REACH - 1 - step), dx)
-        part[rows, :] = part[rows, :] + (forward if way == 1 else backward)[i]
-
-    def collect_all(dx):
-        for way in (1, -1):
-            rs[REACH - 1, dx, way].wait_recv()
-        straight[1 - dx].wait_recv()
-        i = dx * REACH + REACH - 1
-        rows = rows_of(0, dx)
-        part[rows, :] = part[rows, :] + forward[i] + (backward[i] + opposite[dx])
+        cross.append(copy)
 
     row = lax.broadcasted_iota(jnp.int32, (BLOCK, BLOCK), 0)
     lane = lax.broadcasted_iota(jnp.int32, (BLOCK, BLOCK), 1)
@@ -178,39 +146,28 @@
             ).astype(jnp.bfloat16)
             qfull[half, rows, LATENT:] = queries_v[half, :, at + NOPE : at + NOPE + ROPE]
 
-    def fill(step):
-        if step == 0:
-            bounds()
-        elif step == 1:
-            loads[2].wait()
-            loads[3].wait()
-            absorb(0)
-        else:
-            absorb(1)
-
     @pl.when(y == 0)
     def _():
         keys[0, SLOT[0]] = jnp.zeros((BLOCK, KEY), jnp.bfloat16)
         keys[0, SLOT[4]] = jnp.zeros((BLOCK, KEY), jnp.bfloat16)
 
-    for step in range(REACH - 1):
-        fill(step)
-        for dx in (1, 0):
-            for way in (1, -1):
-                collect(step, dx, way)
-                rs[step + 1, dx, way] = pass_on(step + 1, dx, way)
-    fill(REACH - 1)
-    collect_all(1)
-    cross = pltpu.make_async_remote_copy(
-        src_ref=part.at[rows_of(0, 1), :],
-        dst_ref=crossed,
-        send_sem=cross_sem.at[0],
-        recv_sem=cross_sem.at[1],
-        device_id=(ctx, head_peer(0, 1)),
-        device_id_type=MESH,
-    )
-    cross.start()
-    collect_all(0)
+    bounds()
+    rs = []
+    for i, dz in enumerate(ALONG):
+        cross[i].wait_recv()
+        rows = rows_of(dz, 0)
+        part[rows, :] = part[rows, :] + crossed[i]
+        if dz != 0:
+            copy = pltpu.make_async_remote_copy(
+                src_ref=part.at[rows, :],
+                dst_ref=arrived.at[i],
+                send_sem=rs_send.at[i],
+                recv_sem=rs_recv.at[i],
+                device_id=(ctx, head_peer(dz, 0)),
+                device_id_type=MESH,
+            )
+            copy.start()
+            rs.append(copy)
     for i in (6, 7, 8):
         loads[i].wait()
     key_block = (1 - head // 8) * ctx + head // 8 * (63 - ctx)
@@ -222,8 +179,10 @@
     cosine = cos_a * cos_b - sin_a * sin_b
     sine = sin_a * cos_b + cos_a * sin_b
 
-    cross.wait_recv()
-    latent = part[rows_of(0, 0), :] + crossed[...]
+    latent = part[rows_of(0, 0), :]
+    for i, copy in enumerate(rs):
+        copy.wait_recv()
+        latent = latent + arrived[i]
     compressed = latent[:, :LATENT]
     variance = jnp.mean(compressed * compressed, axis=1, keepdims=True)
     normed = compressed * lax.rsqrt(variance + 1e-06) * gain_v[...]
@@ -238,32 +197,37 @@
     ).astype(jnp.bfloat16)
 
     ag = []
-    for i, (dz, dx) in enumerate(OFFSETS):
+
+    def spread(of_head, to_head):
         copy = pltpu.make_async_remote_copy(
-            src_ref=piece(head),
-            dst_ref=piece(head),
-            send_sem=ag_send.at[i],
-            recv_sem=ag_recv.at[head],
-            device_id=(ctx, head_peer(dz, dx)),
+            src_ref=piece(of_head),
+            dst_ref=piece(of_head),
+            send_sem=ag_send.at[len(ag)],
+            recv_sem=ag_recv.at[of_head],
+            device_id=(ctx, to_head),
             device_id_type=MESH,
         )
         copy.start()
         ag.append(copy)
 
-    def gathered(half, part_index):
-        for i in range(CHUNK // ROWS):
-            of_head = half * 8 + part_index * (CHUNK // ROWS) + i
-
-            @pl.when(head != of_head)
-            def _():
-                pltpu.make_async_remote_copy(
-                    src_ref=piece(of_head),
-                    dst_ref=piece(of_head),
-                    send_sem=ag_send.at[0],
-                    recv_sem=ag_recv.at[of_head],
-                    device_id=(ctx, head_peer(1, 0)),
-                    device_id_type=MESH,
-                ).wait_recv()
+    def got(dz, dx):
+        of_head = head_peer(dz, dx)
+        pltpu.make_async_remote_copy(
+            src_ref=piece(of_head),
+            dst_ref=piece(of_head),
+            send_sem=ag_send.at[0],
+            recv_sem=ag_recv.at[of_head],
+            device_id=(ctx, head_peer(1, 0)),
+            device_id_type=MESH,
+        ).wait_recv()
+
+    for dz, dx in NEAR:
+        spread(head, head_peer(dz, dx))
+
+    loads[2].wait()
+    loads[3].wait()
+    absorb(0)
+    absorb(1)
 
     sent = []
 
@@ -331,54 +295,87 @@
         )
 
     onward = y > 0
-    for u in range(PARTS):
-        gathered(0, u)
-        send(None, 0, SLOT[8], u, last, SLOT[4], next_ctx, next_head)
-        send(x_lo == 0, 0, SLOT[8], u, 0, SLOT[6], across_ctx, down_head)
-        send(core == 0, 0, SLOT[8], u, 0, SLOT[7], mate_ctx, head)
-    for u in range(PARTS):
-        gathered(1, u)
-        send(onward, 1, SLOT[8], u, 1, SLOT[4], ctx - 4, head)
-        send(x_lo == 1, 1, SLOT[8], u, 1, SLOT[6], across_ctx, down_head)
-        send(core == 1, 1, SLOT[8], u, 1, SLOT[7], mate_ctx, head)
+    toward = 1 - 2 * (z % 2)
+
+    def pair(steps):
+        which = (z // 2 + steps + 4) % 4
+        return which // 2, which % 2
+
+    own_pair, near_pair, middle_pair, far_pair = pair(0), pair(-toward), pair(toward), pair(2)
+
+    def along_y(half, slot, u, to_slot):
+        send(
+            (half == 0) | onward,
+            half, slot, u,
+            half + (1 - half) * last, to_slot,
+            (1 - half) * next_ctx + half * (ctx - 4), (1 - half) * next_head + half * head,
+        )
+
+    def unturned(half):
+        return (half == 0) | (last == 0)
+
+    def begin(half, u):
+        along_y(half, SLOT[8], u, SLOT[4])
+        send(x_lo == half, half, SLOT[8], u, half, SLOT[6], across_ctx, down_head)
+        send(core == half, half, SLOT[8], u, half, SLOT[7], mate_ctx, head)
+        send((half == 0) & (last == 1), half, SLOT[8], u, 1, either(x_lo, 2, 6), mate_ctx, head)
+
+    def second(half, u):
+        pl.when((half == 1) | onward)(functools.partial(take, half, SLOT[4], u))
+        along_y(half, SLOT[4], u, SLOT[0])
+        send(unturned(half), half, SLOT[4], u, half, either((x_lo + half) % 2, 2, 6), across_ctx, down_head)
+        send(None, half, SLOT[4], u, half, either((core + half) % 2, 3, 5), mate_ctx, head)
+        send((half == 0) & (last == 1) & (x_lo == 1), half, SLOT[4], u, 1, SLOT[2], mate_ctx, head)
+
+    def third(half, u):
+        pl.when((half == 1) | onward)(functools.partial(take, half, SLOT[0], u))
+        send((x_lo != half) & unturned(half), half, SLOT[0], u, half, SLOT[2], across_ctx, down_head)
+        send(core != half, half, SLOT[0], u, half, SLOT[1], mate_ctx, head)
+
+    def across(half, u, slot, first, other):
+        take(half, slot, u)
+        send(None, half, slot, u, half, either((core + half) % 2, first, other), mate_ctx, head)
+
+    got(0, 1)
+    for dx in (0, 1):
+        got(toward, dx)
+    begin(*own_pair)
+    for dz in (-2, 2):
+        for plane in (0, 1):
+            of_head = (z + dz + 8) % 8 * 2 + plane
+            got(dz, (x_hi + plane) % 2)
+            spread(of_head, head_peer(-dz // 2, 0))
+            if dz == (-2 if plane == 0 else 2):
+                spread(of_head, head_peer(-dz, 0))
+    for dx in (0, 1):
+        got(-toward, dx)
+    begin(*near_pair)
+    for dx in (0, 1):
+        got(3 * toward, dx)
+    begin(*middle_pair)
+    for dx in (0, 1):
+        got(4, dx)
+        got(-3 * toward, dx)
+    begin(*far_pair)
+    order = (own_pair, near_pair, middle_pair, far_pair)
+    second(*order[0])
+    second(*order[1])
     score(SLOT[8], 1)
-
-    for u in range(PARTS):
-        pl.when(onward)(functools.partial(take, 0, SLOT[4], u))
-        send(None, 0, SLOT[4], u, last, SLOT[0], next_ctx, next_head)
-        send(None, 0, SLOT[4], u, 0, either(x_lo, 2, 6), across_ctx, down_head)
-        send(None, 0, SLOT[4], u, 0, either(core, 3, 5), mate_ctx, head)
-        take(1, SLOT[4], u)
-        send(onward, 1, SLOT[4], u, 1, SLOT[0], ctx - 4, head)
-        send(None, 1, SLOT[4], u, 1, either(x_lo, 6, 2), across_ctx, down_head)
-        send(None, 1, SLOT[4], u, 1, either(core, 5, 3), mate_ctx, head)
-    score(SLOT[4], 1)
-
-    for u in range(PARTS):
-        pl.when(onward)(functools.partial(take, 0, SLOT[0], u))
-        send(x_lo == 1, 0, SLOT[0], u, 0, SLOT[2], across_ctx, down_head)
-        send(core == 1, 0, SLOT[0], u, 0, SLOT[1], mate_ctx, head)
-        take(1, SLOT[0], u)
-        send(x_lo == 0, 1, SLOT[0], u, 1, SLOT[2], across_ctx, down_head)
-        send(core == 0, 1, SLOT[0], u, 1, SLOT[1], mate_ctx, head)
-    for u in range(PARTS):
-        for half in range(2):
-            take(half, SLOT[6], u)
-            to = either(core, 5, 7) if half == 0 else either(core, 7, 5)
-            send(None, half, SLOT[6], u, half, to, mate_ctx, head)
-    score(SLOT[0], 2)
+    second(*order[2])
+    second(*order[3])
+    for which in order:
+        third(*which)
+    for which in order:
+        across(*which, SLOT[6], 5, 7)
+    score(SLOT[4], 3)
     for half in range(2):
         top = jnp.max(rowmax[half], axis=1, keepdims=True)
         top_early[half] = jnp.broadcast_to(top, (heads * BLOCK, BLOCK))
         total_early[half], mixing[half] = weigh(
             half, 0, EARLY, top, jnp.zeros((heads * BLOCK, BLOCK), jnp.float32)
         )
-
-    for u in range(PARTS):
-        for half in range(2):
-            take(half, SLOT[2], u)
-            to = either(core, 1, 3) if half == 0 else either(core, 3, 1)
-            send(None, half, SLOT[2], u, half, to, mate_ctx, head)
+    for which in order:
+        across(*which, SLOT[2], 1, 3)
     for index in (7, 5):
         for half in range(2):
             for u in range(PARTS):
@@ -402,7 +399,7 @@
                 mixed[n * BLOCK : (n + 1) * BLOCK], w_val_v[n], preferred_element_type=jnp.float32
             ).astype(jnp.bfloat16)
 
-    for copy in [*rs.values(), *straight, cross, *ag]:
+    for copy in [*cross, *rs, *ag]:
         copy.wait_send()
     for condition, copy in sent:
         if condition is None:
@@ -441,10 +438,8 @@
             pltpu.VMEM(turn_block.shape, f32),
             pltpu.VMEM(turn_row.shape, f32),
             pltpu.VMEM((2 * BLOCK, KEY), f32),
-            pltpu.VMEM((2 * REACH, ROWS, KEY), f32),
-            pltpu.VMEM((2 * REACH, ROWS, KEY), f32),
-            pltpu.VMEM((2, ROWS, KEY), f32),
-            pltpu.VMEM((ROWS, KEY), f32),
+            pltpu.VMEM((len(ALONG), ROWS, KEY), f32),
+            pltpu.VMEM((len(ALONG) - 1, ROWS, KEY), f32),
             pltpu.VMEM((2, SPAN, BLOCK, KEY), bf16),
             pltpu.VMEM((2, heads * BLOCK, KEY), bf16),
             pltpu.VMEM((2, SPAN, heads * BLOCK, BLOCK), f32),
@@ -454,8 +449,8 @@
             pltpu.VMEM((2, heads * BLOCK, BLOCK), f32),
             pltpu.VMEM((2, heads * BLOCK, BLOCK), f32),
             pltpu.VMEM((2, heads * BLOCK, LATENT), f32),
-            dma((9,)), dma((2 * REACH,)), dma((2 * REACH,)), dma((2 * REACH,)), dma((2 * REACH,)), dma((2,)), dma((2,)), dma((2,)),
-            dma((PEERS,)), dma((PEERS + 1,)), dma((40,)), dma((2, SPAN, PARTS)),
+            dma((9,)), dma((8,)), dma((8,)), dma((7,)), dma((7,)),
+            dma((PEERS,)), dma((PEERS + 1,)), dma((48,)), dma((2, SPAN, PARTS)),
         ],
         compiler_params=pltpu.CompilerParams(
             collective_id=0, has_side_effects=True, vmem_limit_bytes=60 * 1024 * 1024

time: 57.2 us -> 54.1 us (0.946)
  Pallas kernels: 55.4 us -> 52.2 us
    pallas_call x1, Pallas kernels: 55.4 us -> 52.2 us  [on_device(): pl.pallas_call(body, out_shape=jax.ShapeDtypeStruct((2, BLOCK, heads * VD...]
where the time goes in v4:
time: 54.1 us; the launch traced here: 53.9 us
  Pallas kernels  52.2 us (96%)
  local copies, waits for them, and re-layouts  1.67 us (3%)
    pallas_call x1, Pallas kernels, on_device(): pl.pallas_call(body, out_shape=jax.ShapeDtypeStruct((2, BLOCK, heads * VD...  52.2 us
    unnamed x1, local copies, waits for them, and re-layouts  1.67 us

profile of v4, /device:TPU:19, one launch (start us, length us, event | category | flops | bytes accessed | tf_op | source)
XLA Modules:
  0.0 53.9 jit_solution(3654355353323115309)
XLA Ops:
  0.0 52.2 %shard_map.91 = bf16[2,128,512]{2,1,0:T(8,128)(2,1)} custom-call(bf16[2,448,128]{2,1,0:T(8,128)(2,1)} %bitcast.2, bf16[2,128,768]{2,1,0:T(8,128)(2,1)} %queries_hbm.1, bf16[448,576]{1,0:T(8,128)(2,1)} %w_dkv_hbm.1, f32[1,512]{1,0:T(1,128)} %bitcast.3, bf16[4,512,128]{2,1,0:T(8,128)(2,1)} %w_key_hbm.1, bf16[4,512,128]{2,1,0:T(8,128)(2,1)} %w_val_hbm.1, ...), custom_call_target="tpu_custom_call" | custom-call | tf_op jit(solution)/shard_map/pallas_call | solution.py:425
  52.3 1.7 %copy.11 = bf16[2,128,512]{2,1,0:T(8,128)(2,1)} copy(bf16[2,128,512]{2,1,0:T(8,128)(2,1)} %shard_map.91) | data formatting | bytes 524288

commit v5 on v4

--- a/solution.py
+++ b/solution.py
@@ -31,9 +31,10 @@
 
 def body(
     hidden_hbm, queries_hbm, w_dkv_hbm, gain_hbm, w_key_hbm, w_val_hbm, docs_hbm, turn_block_hbm, turn_row_hbm,
-    out_ref,
+    out_hbm,
     hidden_v, queries_v, w_dkv_v, gain_v, w_key_v, w_val_v, docs_s, turn_block_v, turn_row_v,
-    part, crossed, arrived, keys, qfull, scores, rowmax, lower, probs, top_early, total_early, mixing,
+    part, crossed, arrived, keys, qfull, scores, rowmax, lower, probs, top_early, total_early, mixing, result,
+    out_sem,
     load_sem, cross_send, cross_recv, rs_send, rs_recv, ag_send, ag_recv, win_send, win_recv,
 ):
     ctx = lax.axis_index("ctx")
@@ -363,19 +364,26 @@
     score(SLOT[8], 1)
     second(*order[2])
     second(*order[3])
-    for which in order:
-        third(*which)
-    for which in order:
-        across(*which, SLOT[6], 5, 7)
-    score(SLOT[4], 3)
+    third(*order[0])
+    third(*order[1])
+    across(*order[0], SLOT[6], 5, 7)
+    across(*order[1], SLOT[6], 5, 7)
+    score(SLOT[4], 1)
+    third(*order[2])
+    third(*order[3])
+    across(*order[2], SLOT[6], 5, 7)
+    across(*order[3], SLOT[6], 5, 7)
+    across(*order[0], SLOT[2], 1, 3)
+    across(*order[1], SLOT[2], 1, 3)
+    score(SLOT[0], 2)
     for half in range(2):
         top = jnp.max(rowmax[half], axis=1, keepdims=True)
         top_early[half] = jnp.broadcast_to(top, (heads * BLOCK, BLOCK))
         total_early[half], mixing[half] = weigh(
             half, 0, EARLY, top, jnp.zeros((heads * BLOCK, BLOCK), jnp.float32)
         )
-    for which in order:
-        across(*which, SLOT[2], 1, 3)
+    across(*order[2], SLOT[2], 1, 3)
+    across(*order[3], SLOT[2], 1, 3)
     for index in (7, 5):
         for half in range(2):
             for u in range(PARTS):
@@ -388,6 +396,7 @@
     score(SLOT[1], 2)
 
     loads[4].wait()
+    outs = []
     for half in range(2):
         top = jnp.max(rowmax[half], axis=1, keepdims=True)
         fade = jnp.exp2((top_early[half] - top) * to_log2)
@@ -395,10 +404,16 @@
         numerator = numerator + mixing[half] * fade[:, :1]
         mixed = (numerator * (1.0 / jnp.sum(total, axis=1, keepdims=True))).astype(jnp.bfloat16)
         for n in range(heads):
-            out_ref[half, :, n * VDIM : (n + 1) * VDIM] = jnp.dot(
+            result[half, :, n * VDIM : (n + 1) * VDIM] = jnp.dot(
                 mixed[n * BLOCK : (n + 1) * BLOCK], w_val_v[n], preferred_element_type=jnp.float32
             ).astype(jnp.bfloat16)
 
+        out_copy = pltpu.make_async_copy(result.at[half], out_hbm.at[half], out_sem.at[half])
+        out_copy.start()
+        outs.append(out_copy)
+
+    for copy in outs:
+        copy.wait()
     for copy in [*cross, *rs, *ag]:
         copy.wait_send()
     for condition, copy in sent:
@@ -419,14 +434,13 @@
     turn_block = jnp.asarray(turns(np.arange(64) * BLOCK))
     turn_row = jnp.asarray(turns(np.arange(BLOCK)))
     any_space = pl.BlockSpec(memory_space=pl.ANY)
-    in_vmem = pl.BlockSpec(memory_space=pltpu.VMEM)
     bf16, f32 = jnp.bfloat16, jnp.float32
     dma = pltpu.SemaphoreType.DMA
     return pl.pallas_call(
         body,
         out_shape=jax.ShapeDtypeStruct((2, BLOCK, heads * VDIM), bf16),
         in_specs=[any_space] * 9,
-        out_specs=in_vmem,
+        out_specs=any_space,
         scratch_shapes=[
             pltpu.VMEM(hidden.shape, bf16),
             pltpu.VMEM(queries.shape, bf16),
@@ -449,6 +463,8 @@
             pltpu.VMEM((2, heads * BLOCK, BLOCK), f32),
             pltpu.VMEM((2, heads * BLOCK, BLOCK), f32),
             pltpu.VMEM((2, heads * BLOCK, LATENT), f32),
+            pltpu.VMEM((2, BLOCK, heads * VDIM), bf16),
+            dma((2,)),
             dma((9,)), dma((8,)), dma((8,)), dma((7,)), dma((7,)),
             dma((PEERS,)), dma((PEERS + 1,)), dma((48,)), dma((2, SPAN, PARTS)),
         ],

time: 54.1 us -> 54 us (level)
  no operation moved by 1% of the time
where the time goes in v5:
time: 54 us; the launch traced here: 53.9 us
  Pallas kernels  52.2 us (97%)
  local copies, waits for them, and re-layouts  1.67 us (3%)
    pallas_call x1, Pallas kernels, on_device(): pl.pallas_call(body, out_shape=jax.ShapeDtypeStruct((2, BLOCK, heads * VD...  52.2 us
    unnamed x1, local copies, waits for them, and re-layouts  1.67 us

profile of v5, /device:TPU:19, one launch (start us, length us, event | category | flops | bytes accessed | tf_op | source)
XLA Modules:
  0.0 53.9 jit_solution(2128234528521602693)
XLA Ops:
  0.0 52.2 %shard_map.91 = bf16[2,128,512]{2,1,0:T(8,128)(2,1)} custom-call(bf16[2,448,128]{2,1,0:T(8,128)(2,1)} %bitcast.2, bf16[2,128,768]{2,1,0:T(8,128)(2,1)} %queries_hbm.1, bf16[448,576]{1,0:T(8,128)(2,1)} %w_dkv_hbm.1, f32[1,512]{1,0:T(1,128)} %bitcast.3, bf16[4,512,128]{2,1,0:T(8,128)(2,1)} %w_key_hbm.1, bf16[4,512,128]{2,1,0:T(8,128)(2,1)} %w_val_hbm.1, ...), custom_call_target="tpu_custom_call" | custom-call | tf_op jit(solution)/shard_map/pallas_call | solution.py:439
  52.2 1.7 %copy.11 = bf16[2,128,512]{2,1,0:T(8,128)(2,1)} copy(bf16[2,128,512]{2,1,0:T(8,128)(2,1)} %shard_map.91) | data formatting | bytes 524288
